TPU v7x, 32 devices: a whole 2x2x4 slice. The times are simulated.
32 devices in a mesh: groups: 2 (over x), coarse: 2 (over core), fine: 8 (over z, y).
Axes of the slice: x: 2, y: 2, z: 4, core: 2. Of those that a mesh axis runs over, the one named last changes fastest.
Arguments:
- amplitudes: float32 [32, 4], P(('groups', 'coarse', 'fine')), parts along dimension 0, may hold values from -1 to 1
- control_index: int32 [32, 4], P(('groups', 'coarse', 'fine')), parts along dimension 0, may hold values from 0 to 7
- controls: float32 [8, 512, 512], replicated, may hold values from -0.25 to 0.25
- drift_term: float32 [512, 512], replicated, may hold values from -0.25 to 0.25
- target: float32 [1024, 512], P('groups'), parts along dimension 0, may hold values from -1.5 to 1.5
Outputs:
- gradient: float32 [32, 4], P(('groups', 'coarse', 'fine')), parts along dimension 0
There are 2 independent parts, one for each index of `groups`. A program takes and returns all parts, laid end to end along the dimension named above; an argument that names none is the same for every part. Nothing has to cross between parts.
All inputs are finite; a program needn't handle non-finite values.
Results may differ from a plain program's by a relative error of at most 0.0003.
Values sent between devices are 32-bit elements; how exact they have to be, the bound alone decides.
No kernel may reach another device: no remote copies, remote signals or barrier semaphores. Data moves between devices by JAX's collectives and lax.ppermute only.
A program may use at most 192 MiB of HBM per device.

v0:
```python
import functools

import jax
import jax.numpy as jnp
from jax import lax
from jax.experimental import pallas as pl
from jax.experimental.pallas import tpu as pltpu
from jax.sharding import PartitionSpec as P

step_scale = 0.3
f32 = jnp.float32
bf16 = jnp.bfloat16
SMEM = pl.BlockSpec(memory_space=pltpu.SMEM)
VMEM = pl.BlockSpec(memory_space=pltpu.VMEM)
HBM = pl.BlockSpec(memory_space=pltpu.HBM)


def split(x):
    high = x.astype(bf16)
    return high, (x - high.astype(f32)).astype(bf16)


def dot(a, b):
    return jnp.dot(a, b, preferred_element_type=f32)


def dot_nt(a, b):
    return lax.dot_general(a, b, (((1,), (1,)), ((), ())), preferred_element_type=f32)


def pieces(m, size):
    size = size if m % size == 0 else m
    return [slice(at, at + size) for at in range(0, m, size)]


def dot3(ah, al, bh, bl, cols, rows=slice(None)):
    return (
        dot(ah[rows, :], bh[:, cols])
        + dot(ah[rows, :], bl[:, cols])
        + dot(al[rows, :], bh[:, cols])
    )


def generator(amps, picks, table, drift, s):
    m = drift.shape[0]
    half = step_scale * 0.5
    for rs in pieces(m, 32):
        total = drift[rs, :]
        for amp, pick in zip(amps, picks):
            total = total + amp * table[pick, rs, :]
        s.mix[rs, :] = total
    for i, ti in enumerate(pieces(m, 128)):
        for tj in pieces(m, 128)[: i + 1]:
            value = half * (s.mix[ti, tj] - s.mix[tj, ti].T)
            s.a32[ti, tj] = value
            s.ah[ti, tj], s.al[ti, tj] = split(value)
            if ti != tj:
                back = -value.T
                s.a32[tj, ti] = back
                s.ah[tj, ti], s.al[tj, ti] = split(back)


def mirrored(ah, al, bh, bl, sign, put):
    m = ah.shape[0]
    for cs in pieces(m, 256):
        value = dot3(ah, al, bh, bl, cs, slice(cs.start, m))
        put(slice(cs.start, m), cs, value)
        width = cs.stop - cs.start
        for rs in pieces(m, 256):
            if rs.start > cs.start:
                at = rs.start - cs.start
                flipped = value[at : at + width, :].T
                put(cs, rs, flipped if sign > 0 else -flipped)


def square_step(s):
    def put(rows, cols, value):
        s.b32[rows, cols] = value
        s.bh[rows, cols], s.bl[rows, cols] = split(value)

    mirrored(s.ah, s.al, s.ah, s.al, 1, put)


def cube_step(s):
    def put(rows, cols, value):
        s.dh[rows, cols], s.dl[rows, cols] = split(value)
        a, b = s.a32[rows, cols], s.b32[rows, cols]
        rest = a * (1 / 24) + b * (1 / 120) + value * (1 / 720)
        s.qh[rows, cols], s.ql[rows, cols] = split(rest)
        s.a32[rows, cols] = a + b * 0.5 + value * (1 / 6)

    mirrored(s.ah, s.al, s.bh, s.bl, -1, put)


def last_step(s, wh, wl):
    for cs in pieces(s.ah.shape[0], 256):
        value = dot3(s.dh, s.dl, s.qh, s.ql, cs) + s.a32[:, cs]
        wh[:, cs], wl[:, cs] = split(value)


def inside(x):
    return pltpu.with_memory_space_constraint(x, pltpu.VMEM)


def outside(x):
    return pltpu.with_memory_space_constraint(x, pltpu.HBM)


class Work:
    names = ("mix", "a32", "b32", "ah", "al", "bh", "bl", "dh", "dl", "qh", "ql")

    def __init__(self, refs):
        for name, ref in zip(self.names, refs):
            setattr(self, name, ref)

    @classmethod
    def shapes(cls, m):
        return [pltpu.VMEM((m, m), f32)] * 3 + [pltpu.VMEM((m, m), bf16)] * 8


def propagators(rows, picked, table, works, wh, wl, first):
    count = rows.shape[1] // 2
    drift = table.at[table.shape[0] - 1]
    for row, s in zip(picked, works):
        amps = [rows[row, c] for c in range(count)]
        picks = [rows[row, count + c].astype(jnp.int32) for c in range(count)]
        generator(amps, picks, table, drift, s)
    for s in works:
        square_step(s)
    for s in works:
        cube_step(s)
    for k, (row, s) in enumerate(zip(picked, works)):
        slot = k if first is None else first + row
        last_step(s, wh.at[slot], wl.at[slot])


def first_kernel(amps, picks, controls, drift, table, wh, wl, mine, *scratch):
    sems = scratch[-1]
    kinds, count = controls.shape[0], amps.shape[1]
    own = [pltpu.make_async_copy(drift, mine.at[count], sems.at[count])]
    for c in range(count):
        own.append(pltpu.make_async_copy(controls.at[picks[0, c]], mine.at[c], sems.at[c]))
    rest = [pltpu.make_async_copy(drift, table.at[kinds], sems.at[count + 1 + kinds])]
    for k in range(kinds):
        rest.append(pltpu.make_async_copy(controls.at[k], table.at[k], sems.at[count + 1 + k]))
    for copy in own + rest:
        copy.start()
    for copy in own:
        copy.wait()
    s = Work(scratch[:-1])
    generator([amps[0, c] for c in range(count)], list(range(count)), mine, mine.at[count], s)
    square_step(s)
    cube_step(s)
    last_step(s, wh.at[0], wl.at[0])
    for copy in rest:
        copy.wait()


def build_kernel(first, rows, table, wh_in, wl_in, wh, wl, *scratch):
    size = len(Work.names)
    slots = rows.shape[0]
    works = [Work(scratch[n * size : (n + 1) * size]) for n in range(len(scratch) // size)]
    for n in range(0, slots, len(works)):
        propagators(rows, range(n, n + len(works)), table, works, wh, wl, first)


def chain_kernel(order, place, rows, table, wh_in, wl_in, run, local, wh, wl, rh, rl, both, *scratch):
    size = len(Work.names)
    works = [Work(scratch[n * size : (n + 1) * size]) for n in range(2)]
    m = run.shape[0]
    fine = place[1]
    first = order - rows.shape[0]

    def pair(n, carry):
        propagators(rows, [2 * n, 2 * n + 1], table, works, wh, wl, first)
        return carry

    lax.fori_loop(0, rows.shape[0] // 2, pair, 0)
    start_product(fine, wh.at[fine], wl.at[fine], run, rh, rl)
    for rs in pieces(m, 32):
        both[0, rs, :] = run[rs, :]
    for step in range(1, order):
        slot = step ^ fine
        side = jnp.where(step <= fine, 0, 1)
        for cs in pieces(m, 256):
            value = dot3(wh.at[slot], wl.at[slot], rh, rl, cs) + run[:, cs]
            run[:, cs] = value
            both[side, :, cs] = value
            rh[:, cs], rl[:, cs] = split(value)
    for rs in pieces(m, 32):
        local[rs, :] = both[0, rs, :]


def long_kernel(order, place, rows, table, run, local, wh, wl, rh, rl, *scratch):
    size = len(Work.names)
    works = [Work(scratch[n * size : (n + 1) * size]) for n in range(2)]
    m = run.shape[0]
    fine = place[1]
    for rs in pieces(m, 32):
        value = unit(rs, m)
        run[rs, :] = value
        rh[rs, :], rl[rs, :] = split(value)

    def pair(n, carry):
        steps = [2 * n, 2 * n + 1]
        propagators(rows, [step ^ fine for step in steps], table, works, wh, wl, None)
        for k, step in enumerate(steps):
            for cs in pieces(m, 256):
                value = dot3(wh.at[k], wl.at[k], rh, rl, cs) + run[:, cs]
                run[:, cs] = value
                rh[:, cs], rl[:, cs] = split(value)

            @pl.when(step == fine)
            def _():
                for rs in pieces(m, 32):
                    local[rs, :] = run[rs, :]

        return carry

    lax.fori_loop(0, order // 2, pair, 0)


def unit(rs, m):
    at = lax.broadcasted_iota(jnp.int32, (rs.stop - rs.start, m), 0) + rs.start
    return (at == lax.broadcasted_iota(jnp.int32, (rs.stop - rs.start, m), 1)).astype(f32)


def start_product(fine, wh, wl, run, rh, rl):
    m = run.shape[0]
    for rs in pieces(m, 32):
        value = wh[rs, :].astype(f32) + wl[rs, :].astype(f32) + unit(rs, m)
        run[rs, :] = value
        rh[rs, :], rl[rs, :] = split(value)


def target_kernel(run, target, out, th, tl, bh, bl):
    m = target.shape[0]
    for ti in pieces(m, 128):
        bh[ti, :], bl[ti, :] = split(run[ti, :])
        for tj in pieces(m, 128):
            th[ti, tj], tl[ti, tj] = split(target[tj, ti].T)
    for cs in pieces(m, 256):
        out[:, cs] = dot3(th, tl, bh, bl, cs)


def final_kernel(
    count, place, picks, run, got, turned, th, tl, local, table, out,
    ph, plo, bh, bl, vh, vl, x32, kh, kl, uh, ul, g32,
):
    m = local.shape[0]
    coarse = place[0]

    @pl.when(coarse == 0)
    def _():
        for rs in pieces(m, 32):
            uh[rs, :], ul[rs, :] = split(got[rs, :])
            bh[rs, :], bl[rs, :] = split(run[rs, :])
            ph[rs, :], plo[rs, :] = split(local[rs, :])
        for cs in pieces(m, 256):
            vh[:, cs], vl[:, cs] = split(dot3(th, tl, uh, ul, cs))
        for cs in pieces(m, 256):
            x32[:, cs] = dot3(vh, vl, bh, bl, cs)

    @pl.when(coarse != 0)
    def _():
        for rs in pieces(m, 32):
            bh[rs, :], bl[rs, :] = split(got[rs, :])
            vh[rs, :], vl[rs, :] = split(turned[rs, :])
            uh[rs, :], ul[rs, :] = split(local[rs, :])
        for cs in pieces(m, 256):
            x32[:, cs] = dot3(vh, vl, bh, bl, cs)
        for cs in pieces(m, 256):
            ph[:, cs], plo[:, cs] = split(dot3(uh, ul, bh, bl, cs))

    for i, ti in enumerate(pieces(m, 128)):
        for tj in pieces(m, 128)[: i + 1]:
            value = 0.5 * (x32[tj, ti].T - x32[ti, tj])
            kh[ti, tj], kl[ti, tj] = split(value)
            if ti != tj:
                kh[tj, ti], kl[tj, ti] = split(-value.T)
    for cs in pieces(m, 256):
        uh[:, cs], ul[:, cs] = split(dot3(ph, plo, kh, kl, cs))
    for cs in pieces(m, 256):
        g32[:, cs] = (
            dot_nt(uh[...], ph[cs, :]) + dot_nt(uh[...], plo[cs, :]) + dot_nt(ul[...], ph[cs, :])
        )
    for c in range(count):
        total = jnp.zeros((8, m), f32)
        for rs in pieces(m, 8):
            total = total + table[picks[0, c], rs, :] * g32[rs, :]
        out[0, c] = step_scale * jnp.sum(total)


def on_device(amplitudes, control_index, controls, drift_term, target):
    m = target.shape[0]
    kinds, count = controls.shape[0], amplitudes.shape[1]
    order = lax.axis_size("fine")
    assert amplitudes.shape[0] == 1 and lax.axis_size("coarse") == 2
    assert order & (order - 1) == 0 and order >= 4
    place = jnp.stack([lax.axis_index("coarse"), lax.axis_index("fine")]).astype(jnp.int32)
    square, half = pltpu.VMEM((m, m), f32), pltpu.VMEM((m, m), bf16)
    full = pltpu.VMEM((m, m), f32)
    short = order <= 8

    def params(mib):
        return pltpu.CompilerParams(vmem_limit_bytes=mib << 20)

    def cost(products):
        return pl.CostEstimate(
            flops=6 * products * m**3, bytes_accessed=12 * products * m * m, transcendentals=0
        )

    rows = jnp.concatenate([amplitudes, control_index.astype(f32)], axis=1)
    table = wh = wl = other = None
    bit = 1
    while bit < order:
        swap = [(i, i ^ bit) for i in range(order)]
        coming = lax.ppermute(rows, "fine", swap)
        if bit == 1:
            slots = 8 if short else 1
            slots = min(slots, order)
            halves = pltpu.VMEM((slots, m, m), bf16)
            table, wh, wl = pl.pallas_call(
                first_kernel,
                out_shape=(pltpu.VMEM((kinds + 1, m, m), f32), halves, halves),
                in_specs=[SMEM, SMEM, HBM, HBM],
                out_specs=(VMEM, VMEM, VMEM),
                scratch_shapes=[
                    pltpu.VMEM((count + 1, m, m), f32), *Work.shapes(m),
                    pltpu.SemaphoreType.DMA((count + kinds + 2,)),
                ],
                compiler_params=params(FIRST_MIB),
                cost_estimate=cost(4),
                name="first",
            )(amplitudes, control_index, outside(controls), outside(drift_term))
        elif short:
            width = min(2, bit // 2)
            wh, wl = pl.pallas_call(
                functools.partial(build_kernel, bit // 2),
                out_shape=(halves, halves),
                in_specs=[SMEM, VMEM, VMEM, VMEM],
                out_specs=(VMEM, VMEM),
                scratch_shapes=Work.shapes(m) * width,
                input_output_aliases={2: 0, 3: 1},
                compiler_params=params(BUILD_MIB),
                cost_estimate=cost(4 * bit // 2),
                name="build",
            )(other, *map(inside, (table, wh, wl)))
        other = coming
        rows = jnp.concatenate([rows, other], axis=0)
        bit *= 2

    if short:
        kernel, taken, first = chain_kernel, (other, table, wh, wl), order - other.shape[0]
        outs, aliases = (square, square, halves, halves), {3: 2, 4: 3}
        scratch = [half, half, pltpu.VMEM((2, m, m), f32)]
    else:
        kernel, taken = long_kernel, (rows, table)
        outs, aliases = (square, square), {}
        scratch = [pltpu.VMEM((2, m, m), bf16), pltpu.VMEM((2, m, m), bf16), half, half]
    run, local = pl.pallas_call(
        functools.partial(kernel, order),
        out_shape=outs,
        in_specs=[SMEM, SMEM] + [VMEM] * (len(taken) - 1),
        out_specs=(VMEM,) * len(outs),
        scratch_shapes=[*scratch, *Work.shapes(m) * 2],
        input_output_aliases=aliases,
        compiler_params=params(CHAIN_MIB),
        cost_estimate=cost(23),
        name="chain",
    )(place, taken[0], *map(inside, taken[1:]))[:2]
    got = lax.ppermute(run, "coarse", [(0, 1), (1, 0)])
    turned, th, tl = pl.pallas_call(
        target_kernel,
        out_shape=(square, half, half),
        in_specs=[VMEM, VMEM],
        out_specs=(VMEM, VMEM, VMEM),
        scratch_shapes=[half] * 2,
        compiler_params=params(TURN_MIB),
        cost_estimate=cost(1),
        name="turn",
    )(run, target)
    return pl.pallas_call(
        functools.partial(final_kernel, count),
        out_shape=jax.ShapeDtypeStruct((1, count), f32),
        in_specs=[SMEM, SMEM] + [VMEM] * 7,
        out_specs=SMEM,
        scratch_shapes=[half, half, half, half, half, half, full, half, half, half, half, full],
        compiler_params=params(FINAL_MIB),
        name="final",
    )(place, control_index, run, got, *map(inside, (turned, th, tl, local, table)))


FIRST_MIB = 16
BUILD_MIB = 16
CHAIN_MIB = 20
TURN_MIB = 6
FINAL_MIB = 12


def solution(mesh):
    placed = (
        P(("groups", "coarse", "fine"), None),
        P(("groups", "coarse", "fine"), None),
        P(),
        P(),
        P("groups", None),
    )
    return jax.shard_map(
        on_device,
        mesh=mesh,
        in_specs=placed,
        out_specs=P(("groups", "coarse", "fine"), None),
        check_vma=False,
    )
```

profile of v0, /device:TPU:1, one launch (start us, length us, event | category | flops | bytes accessed | tf_op | source)
XLA Modules:
  0.0 54.6 jit_solution(17006463417253378866)
XLA Ops:
  0.0 0.7 %convert_element_type.3 = f32[1,4]{1,0:T(1,128)S(1)} convert(s32[1,4]{1,0:T(1,128)} %picks.3) | non-fusion elementwise | flops 4 | bytes 32 | tf_op jit(solution)/shard_map/convert_element_type | solution.py:313
  0.7 0.7 %pad_maximum_fusion.2 = f32[1,8]{1,0:T(1,128)S(1)} fusion(f32[1,4]{1,0:T(1,128)S(1)} %convert_element_type.3, f32[1,4]{1,0:T(1,128)} %amps.1), kind=kLoop, calls=%fused_computation.3 | loop fusion | flops 8 | bytes 64 | tf_op jit(solution)/shard_map/concatenate | solution.py:313
  1.4 2.1 %collective-permute-start = (f32[1,8]{1,0:T(1,128)S(1)}, f32[1,8]{1,0:T(1,128)S(1)}, u32[]{:S(2)}, u32[]{:S(2)}) collective-permute-start(f32[1,8]{1,0:T(1,128)S(1)} %pad_maximum_fusion.2), channel_id=1, source_target_pairs={{0,1},{1,0},{2,3},{3,2},{4,5},{5,4},{6,7},{7,6},{8,9},{9,8},{10,11... | collective-permute-start | bytes 104 | tf_op jit(solution)/shard_map/ppermute | solution.py:318
  3.4 0.1 pad_add_fusion.place
  3.5 0.7 %copy-done = f32[1,4]{1,0:T(1,128)S(1)} copy-done((f32[1,4]{1,0:T(1,128)S(1)}, f32[1,4]{1,0:T(1,128)}, u32[]{:S(2)}) %copy-start) | copy-done | bytes 40
  4.2 0.7 %copy-done.1 = s32[1,4]{1,0:T(1,128)S(1)} copy-done((s32[1,4]{1,0:T(1,128)S(1)}, s32[1,4]{1,0:T(1,128)}, u32[]{:S(2)}) %copy-start.1) | copy-done | bytes 40
  4.8 7.8 %first.1 = (f32[9,512,512]{2,1,0:T(8,128)S(1)}, bf16[8,512,512]{2,1,0:T(8,128)(2,1)S(1)}, bf16[8,512,512]{2,1,0:T(8,128)(2,1)S(1)}) custom-call(f32[1,4]{1,0:T(1,128)S(1)} %copy-done, s32[1,4]{1,0:T(1,128)S(1)} %copy-done.1, f32[8,512,512]{2,1,0:T(8,128)} %controls.1, f32[512,512]{1,0:T(8,128)} %drift.1), custom_call_target="tpu_custom_call" | custom-call | flops 3221225472 | bytes 12582912 | tf_op jit(solution)/shard_map/first/pallas_call | solution.py:323
  12.6 0.0 collective-permute-done.rows
  12.6 0.1 pad_maximum_fusion.1
  12.7 0.5 collective-permute-start.1
  13.2 3.9 %build.2 = (bf16[8,512,512]{2,1,0:T(8,128)(2,1)S(1)}, bf16[8,512,512]{2,1,0:T(8,128)(2,1)S(1)}) custom-call(f32[1,8]{1,0:T(1,128)S(1)} %collective-permute-done.rows, f32[9,512,512]{2,1,0:T(8,128)S(1)} %get-tuple-element.17.table, bf16[8,512,512]{2,1,0:T(8,128)(2,1)S(1)} %get-tuple-element.18.wh_in, ...), custom_call_target="tpu_custom_call", output_to_operand_aliasing={{0}: (2, {}), {1}: (3, {})} | custom-call | flops 3221225472 | bytes 12582912 | tf_op jit(solution)/shard_map/build/pallas_call | solution.py:338
  17.1 0.0 collective-permute-done.1.rows
  17.2 0.1 pad_maximum_fusion
  17.2 2.8 %collective-permute-start.2 = (f32[4,8]{1,0:T(4,128)S(1)}, f32[4,8]{1,0:T(4,128)S(1)}, u32[]{:S(2)}, u32[]{:S(2)}) collective-permute-start(f32[4,8]{1,0:T(4,128)S(1)} %pad_maximum_fusion), channel_id=1, source_target_pairs={{0,4},{1,5},{2,6},{3,7},{4,0},{5,1},{6,2},{7,3},{8,12},{9,13},{10,... | collective-permute-start | bytes 392 | tf_op jit(solution)/shard_map/ppermute | solution.py:318
  20.0 5.9 %build.3 = (bf16[8,512,512]{2,1,0:T(8,128)(2,1)S(1)}, bf16[8,512,512]{2,1,0:T(8,128)(2,1)S(1)}) custom-call(f32[2,8]{1,0:T(2,128)S(1)} %collective-permute-done.1.rows, f32[9,512,512]{2,1,0:T(8,128)S(1)} %get-tuple-element.17.table, bf16[8,512,512]{2,1,0:T(8,128)(2,1)S(1)} %get-tuple-element.20.wh_in, ...), custom_call_target="tpu_custom_call", output_to_operand_aliasing={{0}: (2, {}), {1}: (3, {})} | custom-call | flops 6442450944 | bytes 25165824 | tf_op jit(solution)/shard_map/build/pallas_call | solution.py:338
  25.9 0.0 collective-permute-done.2.rows
  25.9 0.0 copy-start.3
  25.9 0.0 copy-start.2
  25.9 18.7 %chain.1 = (f32[512,512]{1,0:T(8,128)S(1)}, f32[512,512]{1,0:T(8,128)S(1)}, bf16[8,512,512]{2,1,0:T(8,128)(2,1)S(1)}, bf16[8,512,512]{2,1,0:T(8,128)(2,1)S(1)}) custom-call(s32[2]{0:T(128)S(1)} %pad_add_fusion.place, f32[4,8]{1,0:T(4,128)S(1)} %collective-permute-done.2.rows, ...), custom_call_target="tpu_custom_call", output_to_operand_aliasing={{2}: (3, {}), {3}: (4, {})} | custom-call | flops 18522046464 | bytes 72351744 | tf_op jit(solution)/shard_map/chain/pallas_call | solution.py:361
  44.6 2.0 %collective-permute-start.3 = (f32[512,512]{1,0:T(8,128)S(1)}, f32[512,512]{1,0:T(8,128)S(1)}, u32[]{:S(2)}, u32[]{:S(2)}) collective-permute-start(f32[512,512]{1,0:T(8,128)S(1)} %get-tuple-element.24.run), channel_id=1, source_target_pairs={{0,8},{8,0},{1,9},{9,1},{2,10},{10,2},{3,11},{11,3},{4,12},{12,4},... | collective-permute-start | bytes 3145736 | tf_op jit(solution)/shard_map/ppermute | solution.py:372
  46.7 0.0 copy-done.3
  46.7 1.1 %turn.1 = (f32[512,512]{1,0:T(8,128)S(1)}, bf16[512,512]{1,0:T(8,128)(2,1)S(1)}, bf16[512,512]{1,0:T(8,128)(2,1)S(1)}) custom-call(f32[512,512]{1,0:T(8,128)S(1)} %get-tuple-element.24.run, f32[512,512]{1,0:T(8,128)S(1)} %copy-done.3), custom_call_target="tpu_custom_call" | custom-call | flops 805306368 | bytes 3145728 | tf_op jit(solution)/shard_map/turn/pallas_call | solution.py:373
  47.8 1.2 %collective-permute-done.3.got = f32[512,512]{1,0:T(8,128)S(1)} collective-permute-done((f32[512,512]{1,0:T(8,128)S(1)}, f32[512,512]{1,0:T(8,128)S(1)}, u32[]{:S(2)}, u32[]{:S(2)}) %collective-permute-start.3) | collective-permute-done | bytes 1048608 | tf_op jit(solution)/shard_map/ppermute | solution.py:372
  49.0 5.5 %final.1 = f32[1,4]{1,0:T(1,128)} custom-call(s32[2]{0:T(128)S(1)} %pad_add_fusion.place, s32[1,4]{1,0:T(1,128)S(1)} %copy-done.2, f32[512,512]{1,0:T(8,128)S(1)} %get-tuple-element.24.run, f32[512,512]{1,0:T(8,128)S(1)} %collective-permute-done.3.got, f32[512,512]{1,0:T(8,128)S(1)} %get-tuple-element.25.turned, bf16[512,512]{1,0:T(8,128)(2,1)S(1)} %get-tuple-element.26.th, ...), custom_call_target="tpu_custom_call" | custom-call | tf_op jit(solution)/shard_map/final/pallas_call | solution.py:383
  (3 shorter events, 0.0 us)
Async XLA Ops:
  1.4 11.2 %collective-permute-start = (f32[1,8]{1,0:T(1,128)S(1)}, f32[1,8]{1,0:T(1,128)S(1)}, u32[]{:S(2)}, u32[]{:S(2)}) collective-permute-start(f32[1,8]{1,0:T(1,128)S(1)} %pad_maximum_fusion.2), channel_id=1, source_target_pairs={{0,1},{1,0},{2,3},{3,2},{4,5},{5,4},{6,7},{7,6},{8,9},{9,8},{10,11... | collective-permute-start | bytes 104 | tf_op jit(solution)/shard_map/ppermute | solution.py:318
  3.5 0.7 %copy-start = (f32[1,4]{1,0:T(1,128)S(1)}, f32[1,4]{1,0:T(1,128)}, u32[]{:S(2)}) copy-start(f32[1,4]{1,0:T(1,128)} %amps.1) | copy-start | bytes 52
  4.2 0.7 %copy-start.1 = (s32[1,4]{1,0:T(1,128)S(1)}, s32[1,4]{1,0:T(1,128)}, u32[]{:S(2)}) copy-start(s32[1,4]{1,0:T(1,128)} %picks.3) | copy-start | bytes 52
  12.7 4.5 %collective-permute-start.1 = (f32[2,8]{1,0:T(2,128)S(1)}, f32[2,8]{1,0:T(2,128)S(1)}, u32[]{:S(2)}, u32[]{:S(2)}) collective-permute-start(f32[2,8]{1,0:T(2,128)S(1)} %pad_maximum_fusion.1), channel_id=1, source_target_pairs={{0,2},{1,3},{2,0},{3,1},{4,6},{5,7},{6,4},{7,5},{8,10},{9,11},{10,... | collective-permute-start | bytes 200 | tf_op jit(solution)/shard_map/ppermute | solution.py:318
  17.2 8.7 %collective-permute-start.2 = (f32[4,8]{1,0:T(4,128)S(1)}, f32[4,8]{1,0:T(4,128)S(1)}, u32[]{:S(2)}, u32[]{:S(2)}) collective-permute-start(f32[4,8]{1,0:T(4,128)S(1)} %pad_maximum_fusion), channel_id=1, source_target_pairs={{0,4},{1,5},{2,6},{3,7},{4,0},{5,1},{6,2},{7,3},{8,12},{9,13},{10,... | collective-permute-start | bytes 392 | tf_op jit(solution)/shard_map/ppermute | solution.py:318
  25.9 20.8 %copy-start.3 = (f32[512,512]{1,0:T(8,128)S(1)}, f32[512,512]{1,0:T(8,128)}, u32[]{:S(2)}) copy-start(f32[512,512]{1,0:T(8,128)} %target.1) | copy-start | bytes 3145732
  25.9 23.0 %copy-start.2 = (s32[1,4]{1,0:T(1,128)S(1)}, s32[1,4]{1,0:T(1,128)}, u32[]{:S(2)}) copy-start(s32[1,4]{1,0:T(1,128)} %picks.3) | copy-start | bytes 52
  44.6 4.3 %collective-permute-start.3 = (f32[512,512]{1,0:T(8,128)S(1)}, f32[512,512]{1,0:T(8,128)S(1)}, u32[]{:S(2)}, u32[]{:S(2)}) collective-permute-start(f32[512,512]{1,0:T(8,128)S(1)} %get-tuple-element.24.run), channel_id=1, source_target_pairs={{0,8},{8,0},{1,9},{9,1},{2,10},{10,2},{3,11},{11,3},{4,12},{12,4},... | collective-permute-start | bytes 3145736 | tf_op jit(solution)/shard_map/ppermute | solution.py:372
where the time goes:
time: 55.2 us; the launch traced here: 54.6 us
  Pallas kernels  42.8 us (78%)
  starting transfers between devices  7.4 us (13%)
  other arithmetic  1.61 us (3%)
  local copies, waits for them, and re-layouts  1.32 us (2%)
  waiting for transfers between devices  1.17 us (2%)
    pallas_call x1, Pallas kernels, on_device(): pl.pallas_call(functools.partial(kernel, order), out_shape=outs, in_specs...  18.7 us
    pallas_call x2, Pallas kernels, on_device(): pl.pallas_call(functools.partial(build_kernel, bit // 2), out_shape=(halv...  9.81 us
    pallas_call x1, Pallas kernels, on_device(): pl.pallas_call(first_kernel, out_shape=(pltpu.VMEM((kinds + 1, m, m), f32...  7.76 us
    pallas_call x1, Pallas kernels, on_device(): pl.pallas_call(functools.partial(final_kernel, count), out_shape=jax.Shap...  5.47 us
    ppermute x3, starting transfers between devices, on_device(): coming = lax.ppermute(rows, 'fine', swap)  5.36 us
    ppermute x1, starting transfers between devices, on_device(): got = lax.ppermute(run, 'coarse', [(0, 1), (1, 0)])  2.04 us
    unnamed x8, local copies, waits for them, and re-layouts  1.32 us
    ppermute x1, waiting for transfers between devices, on_device(): got = lax.ppermute(run, 'coarse', [(0, 1), (1, 0)])  1.17 us
  transfers between devices with their start and end apart: 4, of which 1 were waited for; matrix products, arithmetic and copies ran while one was open for 0% of the time, Pallas kernels for 34%

commit v1 on v0

--- a/solution.py
+++ b/solution.py
@@ -134,61 +134,116 @@
         last_step(s, wh.at[slot], wl.at[slot])
 
 
-def first_kernel(amps, picks, controls, drift, table, wh, wl, mine, *scratch):
+def first_kernel(rows, controls, drift, table, wh, wl, mine, *scratch):
     sems = scratch[-1]
-    kinds, count = controls.shape[0], amps.shape[1]
+    kinds, count = controls.shape[0], rows.shape[1] // 2
     own = [pltpu.make_async_copy(drift, mine.at[count], sems.at[count])]
     for c in range(count):
-        own.append(pltpu.make_async_copy(controls.at[picks[0, c]], mine.at[c], sems.at[c]))
+        pick = rows[0, count + c].astype(jnp.int32)
+        own.append(pltpu.make_async_copy(controls.at[pick], mine.at[c], sems.at[c]))
     rest = [pltpu.make_async_copy(drift, table.at[kinds], sems.at[count + 1 + kinds])]
     for k in range(kinds):
         rest.append(pltpu.make_async_copy(controls.at[k], table.at[k], sems.at[count + 1 + k]))
-    for copy in own + rest:
+    for copy in own:
         copy.start()
     for copy in own:
         copy.wait()
+    for copy in rest:
+        copy.start()
     s = Work(scratch[:-1])
-    generator([amps[0, c] for c in range(count)], list(range(count)), mine, mine.at[count], s)
+    generator([rows[0, c] for c in range(count)], list(range(count)), mine, mine.at[count], s)
     square_step(s)
     cube_step(s)
-    last_step(s, wh.at[0], wl.at[0])
+    last_step(s, wh, wl)
     for copy in rest:
         copy.wait()
 
 
-def build_kernel(first, rows, table, wh_in, wl_in, wh, wl, *scratch):
-    size = len(Work.names)
-    slots = rows.shape[0]
-    works = [Work(scratch[n * size : (n + 1) * size]) for n in range(len(scratch) // size)]
-    for n in range(0, slots, len(works)):
-        propagators(rows, range(n, n + len(works)), table, works, wh, wl, first)
-
-
-def chain_kernel(order, place, rows, table, wh_in, wl_in, run, local, wh, wl, rh, rl, both, *scratch):
-    size = len(Work.names)
-    works = [Work(scratch[n * size : (n + 1) * size]) for n in range(2)]
-    m = run.shape[0]
+def multiply_on(wh, wl, run, rh, rl):
+    for cs in pieces(run.shape[0], 256):
+        value = dot3(wh, wl, rh, rl, cs) + run[:, cs]
+        run[:, cs] = value
+        rh[:, cs], rl[:, cs] = split(value)
+
+
+def copy_rows(source, goal):
+    for rs in pieces(goal.shape[0], 32):
+        goal[rs, :] = source[rs, :]
+
+
+def chain_kernel(order, place, rows, table, own_h, own_l, run, local, rh, rl, *scratch):
     fine = place[1]
-    first = order - rows.shape[0]
-
-    def pair(n, carry):
-        propagators(rows, [2 * n, 2 * n + 1], table, works, wh, wl, first)
+    drift = table.at[table.shape[0] - 1]
+    count = rows.shape[1] // 2
+    others = order - 1
+    mix, dh, dl, qh, ql = scratch[:5]
+    works, w_refs = [], []
+    for n in range(2):
+        a32, ah, al, b32, bh, bl, wh, wl = scratch[5 + 8 * n : 13 + 8 * n]
+        works.append(Work((mix, a32, b32, ah, al, bh, bl, dh, dl, qh, ql)))
+        w_refs.append((wh, wl))
+
+    def start(n, s):
+        step = jnp.where(n < fine, n, n + 1)
+        row = step ^ fine
+        amps = [rows[row, c] for c in range(count)]
+        picks = [rows[row, count + c].astype(jnp.int32) for c in range(count)]
+        generator(amps, picks, table, drift, s)
+        square_step(s)
+
+    def stage(n, side, more):
+        cube_step(works[side])
+        last_step(works[side], *w_refs[side])
+        if more:
+            start(n + 1, works[1 - side])
+
+    def own():
+        multiply_on(own_h, own_l, run, rh, rl)
+        copy_rows(run, local)
+
+    def advance(n, side):
+        @pl.when(fine == n)
+        def _():
+            own()
+
+        multiply_on(*w_refs[side], run, rh, rl)
+
+    start(0, works[0])
+    stage(0, 0, True)
+
+    @pl.when(fine == 0)
+    def _():
+        start_product(own_h, own_l, run, rh, rl)
+        copy_rows(run, local)
+
+    @pl.when(fine != 0)
+    def _():
+        for rs in pieces(run.shape[0], 32):
+            value = unit(rs, run.shape[0])
+            run[rs, :] = value
+            rh[rs, :], rl[rs, :] = split(value)
+
+    multiply_on(*w_refs[0], run, rh, rl)
+    stage(1, 1, others > 2)
+
+    def two(k, carry):
+        n = 2 * k + 2
+        advance(n - 1, 1)
+        stage(n, 0, True)
+        advance(n, 0)
+        stage(n + 1, 1, True)
         return carry
 
-    lax.fori_loop(0, rows.shape[0] // 2, pair, 0)
-    start_product(fine, wh.at[fine], wl.at[fine], run, rh, rl)
-    for rs in pieces(m, 32):
-        both[0, rs, :] = run[rs, :]
-    for step in range(1, order):
-        slot = step ^ fine
-        side = jnp.where(step <= fine, 0, 1)
-        for cs in pieces(m, 256):
-            value = dot3(wh.at[slot], wl.at[slot], rh, rl, cs) + run[:, cs]
-            run[:, cs] = value
-            both[side, :, cs] = value
-            rh[:, cs], rl[:, cs] = split(value)
-    for rs in pieces(m, 32):
-        local[rs, :] = both[0, rs, :]
+    loops = max(others - 3, 0) // 2
+    lax.fori_loop(0, loops, two, 0)
+    for n in range(2 * loops + 2, others):
+        advance(n - 1, (n - 1) % 2)
+        stage(n, n % 2, n + 1 < others)
+    advance(others - 1, (others - 1) % 2)
+
+    @pl.when(fine == others)
+    def _():
+        own()
 
 
 def long_kernel(order, place, rows, table, run, local, wh, wl, rh, rl, *scratch):
@@ -225,7 +280,7 @@
     return (at == lax.broadcasted_iota(jnp.int32, (rs.stop - rs.start, m), 1)).astype(f32)
 
 
-def start_product(fine, wh, wl, run, rh, rl):
+def start_product(wh, wl, run, rh, rl):
     m = run.shape[0]
     for rs in pieces(m, 32):
         value = wh[rs, :].astype(f32) + wl[rs, :].astype(f32) + unit(rs, m)
@@ -233,12 +288,17 @@
         rh[rs, :], rl[rs, :] = split(value)
 
 
-def target_kernel(run, target, out, th, tl, bh, bl):
+def flip_kernel(rows, target, table, th, tl, table_out):
     m = target.shape[0]
     for ti in pieces(m, 128):
-        bh[ti, :], bl[ti, :] = split(run[ti, :])
         for tj in pieces(m, 128):
             th[ti, tj], tl[ti, tj] = split(target[tj, ti].T)
+
+
+def target_kernel(run, th, tl, out, bh, bl):
+    m = run.shape[0]
+    for rs in pieces(m, 32):
+        bh[rs, :], bl[rs, :] = split(run[rs, :])
     for cs in pieces(m, 256):
         out[:, cs] = dot3(th, tl, bh, bl, cs)
 
@@ -310,20 +370,16 @@
             flops=6 * products * m**3, bytes_accessed=12 * products * m * m, transcendentals=0
         )
 
-    rows = jnp.concatenate([amplitudes, control_index.astype(f32)], axis=1)
-    table = wh = wl = other = None
-    bit = 1
+    rows = lax.optimization_barrier(jnp.concatenate([amplitudes, control_index.astype(f32)], axis=1))
+    bit, parts = 1, []
     while bit < order:
         swap = [(i, i ^ bit) for i in range(order)]
         coming = lax.ppermute(rows, "fine", swap)
         if bit == 1:
-            slots = 8 if short else 1
-            slots = min(slots, order)
-            halves = pltpu.VMEM((slots, m, m), bf16)
             table, wh, wl = pl.pallas_call(
                 first_kernel,
-                out_shape=(pltpu.VMEM((kinds + 1, m, m), f32), halves, halves),
-                in_specs=[SMEM, SMEM, HBM, HBM],
+                out_shape=(pltpu.VMEM((kinds + 1, m, m), f32), half, half),
+                in_specs=[SMEM, HBM, HBM],
                 out_specs=(VMEM, VMEM, VMEM),
                 scratch_shapes=[
                     pltpu.VMEM((count + 1, m, m), f32), *Work.shapes(m),
@@ -332,54 +388,49 @@
                 compiler_params=params(FIRST_MIB),
                 cost_estimate=cost(4),
                 name="first",
-            )(amplitudes, control_index, outside(controls), outside(drift_term))
-        elif short:
-            width = min(2, bit // 2)
-            wh, wl = pl.pallas_call(
-                functools.partial(build_kernel, bit // 2),
-                out_shape=(halves, halves),
-                in_specs=[SMEM, VMEM, VMEM, VMEM],
-                out_specs=(VMEM, VMEM),
-                scratch_shapes=Work.shapes(m) * width,
-                input_output_aliases={2: 0, 3: 1},
-                compiler_params=params(BUILD_MIB),
-                cost_estimate=cost(4 * bit // 2),
-                name="build",
-            )(other, *map(inside, (table, wh, wl)))
-        other = coming
-        rows = jnp.concatenate([rows, other], axis=0)
+            )(rows, outside(controls), outside(drift_term))
+        elif bit == 2:
+            th, tl, table = pl.pallas_call(
+                flip_kernel,
+                out_shape=(half, half, pltpu.VMEM((kinds + 1, m, m), f32)),
+                in_specs=[SMEM, VMEM, VMEM],
+                out_specs=(VMEM, VMEM, VMEM),
+                input_output_aliases={2: 2},
+                compiler_params=params(TURN_MIB),
+                cost_estimate=cost(1),
+                name="flip",
+            )(rows, target, inside(table))
+        rows = jnp.concatenate([rows, coming], axis=0)
         bit *= 2
 
+    outs = (square, square)
     if short:
-        kernel, taken, first = chain_kernel, (other, table, wh, wl), order - other.shape[0]
-        outs, aliases = (square, square, halves, halves), {3: 2, 4: 3}
-        scratch = [half, half, pltpu.VMEM((2, m, m), f32)]
+        kernel, taken = chain_kernel, (rows, table, wh, wl)
+        scratch = [half, half, full] + [half] * 4 + [full, half, half, full, half, half, half, half] * 2
     else:
         kernel, taken = long_kernel, (rows, table)
-        outs, aliases = (square, square), {}
-        scratch = [pltpu.VMEM((2, m, m), bf16), pltpu.VMEM((2, m, m), bf16), half, half]
+        scratch = [pltpu.VMEM((2, m, m), bf16)] * 2 + [half] * 2 + Work.shapes(m) * 2
     run, local = pl.pallas_call(
         functools.partial(kernel, order),
         out_shape=outs,
         in_specs=[SMEM, SMEM] + [VMEM] * (len(taken) - 1),
         out_specs=(VMEM,) * len(outs),
-        scratch_shapes=[*scratch, *Work.shapes(m) * 2],
-        input_output_aliases=aliases,
+        scratch_shapes=scratch,
         compiler_params=params(CHAIN_MIB),
         cost_estimate=cost(23),
         name="chain",
-    )(place, taken[0], *map(inside, taken[1:]))[:2]
+    )(place, taken[0], *map(inside, taken[1:]))
     got = lax.ppermute(run, "coarse", [(0, 1), (1, 0)])
-    turned, th, tl = pl.pallas_call(
+    turned = pl.pallas_call(
         target_kernel,
-        out_shape=(square, half, half),
-        in_specs=[VMEM, VMEM],
-        out_specs=(VMEM, VMEM, VMEM),
+        out_shape=square,
+        in_specs=[VMEM, VMEM, VMEM],
+        out_specs=VMEM,
         scratch_shapes=[half] * 2,
         compiler_params=params(TURN_MIB),
         cost_estimate=cost(1),
         name="turn",
-    )(run, target)
+    )(run, inside(th), inside(tl))
     return pl.pallas_call(
         functools.partial(final_kernel, count),
         out_shape=jax.ShapeDtypeStruct((1, count), f32),
@@ -392,8 +443,7 @@
 
 
 FIRST_MIB = 16
-BUILD_MIB = 16
-CHAIN_MIB = 20
+CHAIN_MIB = 22
 TURN_MIB = 6
 FINAL_MIB = 12
 

time: 55.2 us -> 58 us (1.051)
  starting transfers between devices: 7.4 us -> 9.11 us
  local copies, waits for them, and re-layouts: 1.32 us -> 0.01 us
  waiting for transfers between devices: 1.17 us -> 2.47 us
  Pallas kernels: 42.8 us -> 44 us
    pallas_call x1, Pallas kernels: 18.7 us -> 29.9 us  [on_device(): pl.pallas_call(functools.partial(kernel, order), out_shape=outs, in_specs...]
    pallas_call x3 -> x2, Pallas kernels: 10.9 us -> 1.89 us  [the longest x1 1 us: on_device(): pl.pallas_call(target_kernel, out_shape=square, in_specs=[VMEM, VMEM, VME...]
    unnamed x8 -> x4, local copies, waits for them, and re-layouts: 1.32 us -> 0.01 us
    ppermute x1, starting transfers between devices: 2.04 us -> 3.32 us  [on_device(): got = lax.ppermute(run, 'coarse', [(0, 1), (1, 0)])]
    ppermute x3, waiting for transfers between devices: 0.01 us -> 1.18 us  [on_device(): coming = lax.ppermute(rows, 'fine', swap)]
    pallas_call x1, Pallas kernels: 7.76 us -> 6.86 us  [on_device(): pl.pallas_call(first_kernel, out_shape=(pltpu.VMEM((kinds + 1, m, m), f32...]
  transfers between devices with their start and end apart: 4 -> 4, of which waited for: 1 -> 3; matrix products, arithmetic and copies ran while one was open for 0% -> 0% of each run, Pallas kernels for 34% -> 15%
where the time goes in v1:
time: 58 us; the launch traced here: 57.4 us
  Pallas kernels  44 us (76%)
  starting transfers between devices  9.11 us (16%)
  waiting for transfers between devices  2.47 us (4%)
  other arithmetic  1.58 us (3%)
    pallas_call x1, Pallas kernels, on_device(): pl.pallas_call(functools.partial(kernel, order), out_shape=outs, in_specs...  29.9 us
    pallas_call x1, Pallas kernels, on_device(): pl.pallas_call(first_kernel, out_shape=(pltpu.VMEM((kinds + 1, m, m), f32...  6.86 us
    ppermute x3, starting transfers between devices, on_device(): coming = lax.ppermute(rows, 'fine', swap)  5.79 us
    pallas_call x1, Pallas kernels, on_device(): pl.pallas_call(functools.partial(final_kernel, count), out_shape=jax.Shap...  5.28 us
    ppermute x1, starting transfers between devices, on_device(): got = lax.ppermute(run, 'coarse', [(0, 1), (1, 0)])  3.32 us
    ppermute x1, waiting for transfers between devices, on_device(): got = lax.ppermute(run, 'coarse', [(0, 1), (1, 0)])  1.28 us
    ppermute x3, waiting for transfers between devices, on_device(): coming = lax.ppermute(rows, 'fine', swap)  1.18 us
  transfers between devices with their start and end apart: 4, of which 3 were waited for; matrix products, arithmetic and copies ran while one was open for 0% of the time, Pallas kernels for 15%

profile of v1, /device:TPU:1, one launch (start us, length us, event | category | flops | bytes accessed | tf_op | source)
XLA Modules:
  0.0 57.4 jit_solution(14706213742134007046)
XLA Ops:
  0.0 0.0 copy-start
  0.0 0.7 %convert_element_type.3 = f32[1,4]{1,0:T(1,128)S(1)} convert(s32[1,4]{1,0:T(1,128)} %picks.1) | non-fusion elementwise | flops 4 | bytes 32 | tf_op jit(solution)/shard_map/convert_element_type | solution.py:373
  0.7 0.7 %pad_maximum_fusion.3.rows = f32[1,8]{1,0:T(1,128)S(1)} fusion(f32[1,4]{1,0:T(1,128)S(1)} %convert_element_type.3, f32[1,4]{1,0:T(1,128)} %param.5), kind=kLoop, calls=%fused_computation.4 | loop fusion | flops 8 | bytes 64 | tf_op jit(solution)/shard_map/concatenate | solution.py:373
  1.5 2.1 %collective-permute-start = (f32[1,8]{1,0:T(1,128)S(1)}, f32[1,8]{1,0:T(1,128)S(1)}, u32[]{:S(2)}, u32[]{:S(2)}) collective-permute-start(f32[1,8]{1,0:T(1,128)S(1)} %pad_maximum_fusion.3.rows), channel_id=1, source_target_pairs={{0,1},{1,0},{2,3},{3,2},{4,5},{5,4},{6,7},{7,6},{8,9},{9,8},{10,11... | collective-permute-start | bytes 104 | tf_op jit(solution)/shard_map/ppermute | solution.py:377
  3.5 6.9 %first.1 = (f32[9,512,512]{2,1,0:T(8,128)S(1)}, bf16[512,512]{1,0:T(8,128)(2,1)S(1)}, bf16[512,512]{1,0:T(8,128)(2,1)S(1)}) custom-call(f32[1,8]{1,0:T(1,128)S(1)} %pad_maximum_fusion.3.rows, f32[8,512,512]{2,1,0:T(8,128)} %controls.1, f32[512,512]{1,0:T(8,128)} %drift.1), custom_call_target="tpu_custom_call" | custom-call | flops 3221225472 | bytes 12582912 | tf_op jit(solution)/shard_map/first/pallas_call | solution.py:379
  10.4 0.0 collective-permute-done
  10.4 1.4 %collective-permute-start.1 = (f32[2,8]{1,0:T(2,128)S(1)}, f32[2,8]{1,0:T(2,128)S(1)}, u32[]{:S(2)}, u32[]{:S(2)}) collective-permute-start(f32[2,8]{1,0:T(2,128)S(1)} %pad_maximum_fusion.2.rows), channel_id=1, source_target_pairs={{0,2},{1,3},{2,0},{3,1},{4,6},{5,7},{6,4},{7,5},{8,10},{9,11},{10,... | collective-permute-start | bytes 200 | tf_op jit(solution)/shard_map/ppermute | solution.py:377
  11.8 0.1 pad_add_fusion.place
  11.9 1.1 %collective-permute-done.1 = f32[2,8]{1,0:T(2,128)S(1)} collective-permute-done((f32[2,8]{1,0:T(2,128)S(1)}, f32[2,8]{1,0:T(2,128)S(1)}, u32[]{:S(2)}, u32[]{:S(2)}) %collective-permute-start.1) | collective-permute-done | bytes 96 | tf_op jit(solution)/shard_map/ppermute | solution.py:377
  12.9 2.4 %collective-permute-start.2 = (f32[4,8]{1,0:T(4,128)S(1)}, f32[4,8]{1,0:T(4,128)S(1)}, u32[]{:S(2)}, u32[]{:S(2)}) collective-permute-start(f32[4,8]{1,0:T(4,128)S(1)} %pad_maximum_fusion.1), channel_id=1, source_target_pairs={{0,4},{1,5},{2,6},{3,7},{4,0},{5,1},{6,2},{7,3},{8,12},{9,13},{10,... | collective-permute-start | bytes 392 | tf_op jit(solution)/shard_map/ppermute | solution.py:377
  15.3 0.0 copy-done
  15.3 0.9 %flip.1 = (bf16[512,512]{1,0:T(8,128)(2,1)S(1)}, bf16[512,512]{1,0:T(8,128)(2,1)S(1)}, f32[9,512,512]{2,1,0:T(8,128)S(1)}) custom-call(f32[2,8]{1,0:T(2,128)S(1)} %pad_maximum_fusion.2.rows, f32[512,512]{1,0:T(8,128)S(1)} %copy-done, f32[9,512,512]{2,1,0:T(8,128)S(1)} %get-tuple-element.13.table), custom_call_target="tpu_custom_call", output_to_operand_aliasing={{2}: (2, {})} | custom-call | flops 805306368 | bytes 3145728 | tf_op jit(solution)/shard_map/flip/pallas_call | solution.py:393
  16.2 0.1 collective-permute-done.2
  16.3 0.0 copy-start.1
  16.4 29.9 %chain.1 = (f32[512,512]{1,0:T(8,128)S(1)}, f32[512,512]{1,0:T(8,128)S(1)}) custom-call(s32[2]{0:T(128)S(1)} %pad_add_fusion.place, f32[8,8]{1,0:T(8,128)S(1)} %pad_maximum_fusion.rows, f32[9,512,512]{2,1,0:T(8,128)S(1)} %get-tuple-element.14.table, bf16[512,512]{1,0:T(8,128)(2,1)S(1)} %get-tuple-element.15.own_h, bf16[512,512]{1,0:T(8,128)(2,1)S(1)} %get-tuple-element.16.own_l), custom_call_target="tpu_custom_call" | custom-call | flops 18522046464 | bytes 72351744 | tf_op jit(solution)/shard_map/chain/pallas_call | solution.py:413
  46.3 3.3 %collective-permute-start.3 = (f32[512,512]{1,0:T(8,128)S(1)}, f32[512,512]{1,0:T(8,128)S(1)}, u32[]{:S(2)}, u32[]{:S(2)}) collective-permute-start(f32[512,512]{1,0:T(8,128)S(1)} %get-tuple-element.17.run), channel_id=1, source_target_pairs={{0,8},{8,0},{1,9},{9,1},{2,10},{10,2},{3,11},{11,3},{4,12},{12,4},... | collective-permute-start | bytes 3145736 | tf_op jit(solution)/shard_map/ppermute | solution.py:423
  49.6 1.0 %turn.1.turned = f32[512,512]{1,0:T(8,128)S(1)} custom-call(f32[512,512]{1,0:T(8,128)S(1)} %get-tuple-element.17.run, bf16[512,512]{1,0:T(8,128)(2,1)S(1)} %get-tuple-element.18.th, bf16[512,512]{1,0:T(8,128)(2,1)S(1)} %get-tuple-element.19.tl), custom_call_target="tpu_custom_call" | custom-call | flops 805306368 | bytes 3145728 | tf_op jit(solution)/shard_map/turn/pallas_call | solution.py:424
  50.6 1.3 %collective-permute-done.3.got = f32[512,512]{1,0:T(8,128)S(1)} collective-permute-done((f32[512,512]{1,0:T(8,128)S(1)}, f32[512,512]{1,0:T(8,128)S(1)}, u32[]{:S(2)}, u32[]{:S(2)}) %collective-permute-start.3) | collective-permute-done | bytes 1048608 | tf_op jit(solution)/shard_map/ppermute | solution.py:423
  51.9 0.0 copy-done.1
  51.9 5.3 %final.1 = f32[1,4]{1,0:T(1,128)} custom-call(s32[2]{0:T(128)S(1)} %pad_add_fusion.place, s32[1,4]{1,0:T(1,128)S(1)} %copy-done.1, f32[512,512]{1,0:T(8,128)S(1)} %get-tuple-element.17.run, f32[512,512]{1,0:T(8,128)S(1)} %collective-permute-done.3.got, f32[512,512]{1,0:T(8,128)S(1)} %turn.1.turned, bf16[512,512]{1,0:T(8,128)(2,1)S(1)} %get-tuple-element.18.th, ...), custom_call_target="tpu_custom_call" | custom-call | tf_op jit(solution)/shard_map/final/pallas_call | solution.py:434
  (3 shorter events, 0.0 us)
Async XLA Ops:
  0.0 15.3 %copy-start = (f32[512,512]{1,0:T(8,128)S(1)}, f32[512,512]{1,0:T(8,128)}, u32[]{:S(2)}) copy-start(f32[512,512]{1,0:T(8,128)} %target.1) | copy-start | bytes 3145732
  1.5 8.9 %collective-permute-start = (f32[1,8]{1,0:T(1,128)S(1)}, f32[1,8]{1,0:T(1,128)S(1)}, u32[]{:S(2)}, u32[]{:S(2)}) collective-permute-start(f32[1,8]{1,0:T(1,128)S(1)} %pad_maximum_fusion.3.rows), channel_id=1, source_target_pairs={{0,1},{1,0},{2,3},{3,2},{4,5},{5,4},{6,7},{7,6},{8,9},{9,8},{10,11... | collective-permute-start | bytes 104 | tf_op jit(solution)/shard_map/ppermute | solution.py:377
  10.4 2.5 %collective-permute-start.1 = (f32[2,8]{1,0:T(2,128)S(1)}, f32[2,8]{1,0:T(2,128)S(1)}, u32[]{:S(2)}, u32[]{:S(2)}) collective-permute-start(f32[2,8]{1,0:T(2,128)S(1)} %pad_maximum_fusion.2.rows), channel_id=1, source_target_pairs={{0,2},{1,3},{2,0},{3,1},{4,6},{5,7},{6,4},{7,5},{8,10},{9,11},{10,... | collective-permute-start | bytes 200 | tf_op jit(solution)/shard_map/ppermute | solution.py:377
  12.9 3.4 %collective-permute-start.2 = (f32[4,8]{1,0:T(4,128)S(1)}, f32[4,8]{1,0:T(4,128)S(1)}, u32[]{:S(2)}, u32[]{:S(2)}) collective-permute-start(f32[4,8]{1,0:T(4,128)S(1)} %pad_maximum_fusion.1), channel_id=1, source_target_pairs={{0,4},{1,5},{2,6},{3,7},{4,0},{5,1},{6,2},{7,3},{8,12},{9,13},{10,... | collective-permute-start | bytes 392 | tf_op jit(solution)/shard_map/ppermute | solution.py:377
  16.3 35.6 %copy-start.1 = (s32[1,4]{1,0:T(1,128)S(1)}, s32[1,4]{1,0:T(1,128)}, u32[]{:S(2)}) copy-start(s32[1,4]{1,0:T(1,128)} %picks.1) | copy-start | bytes 52
  46.3 5.6 %collective-permute-start.3 = (f32[512,512]{1,0:T(8,128)S(1)}, f32[512,512]{1,0:T(8,128)S(1)}, u32[]{:S(2)}, u32[]{:S(2)}) collective-permute-start(f32[512,512]{1,0:T(8,128)S(1)} %get-tuple-element.17.run), channel_id=1, source_target_pairs={{0,8},{8,0},{1,9},{9,1},{2,10},{10,2},{3,11},{11,3},{4,12},{12,4},... | collective-permute-start | bytes 3145736 | tf_op jit(solution)/shard_map/ppermute | solution.py:423

commit v2 on v0

--- a/solution.py
+++ b/solution.py
@@ -41,17 +41,24 @@
     )
 
 
-def generator(amps, picks, table, drift, s):
-    m = drift.shape[0]
-    half = step_scale * 0.5
-    for rs in pieces(m, 32):
-        total = drift[rs, :]
-        for amp, pick in zip(amps, picks):
-            total = total + amp * table[pick, rs, :]
-        s.mix[rs, :] = total
+def skewed(ref):
+    m = ref.shape[0]
     for i, ti in enumerate(pieces(m, 128)):
         for tj in pieces(m, 128)[: i + 1]:
-            value = half * (s.mix[ti, tj] - s.mix[tj, ti].T)
+            value = (step_scale * 0.5) * (ref[ti, tj] - ref[tj, ti].T)
+            ref[ti, tj] = value
+            if ti != tj:
+                ref[tj, ti] = -value.T
+
+
+def generator(amps, picks, table, s):
+    kinds = table.shape[0] - 1
+    m = table.shape[1]
+    for i, ti in enumerate(pieces(m, 128)):
+        for tj in pieces(m, 128)[: i + 1]:
+            value = table[kinds, ti, tj]
+            for amp, pick in zip(amps, picks):
+                value = value + amp * table[pick, ti, tj]
             s.a32[ti, tj] = value
             s.ah[ti, tj], s.al[ti, tj] = split(value)
             if ti != tj:
@@ -107,7 +114,7 @@
 
 
 class Work:
-    names = ("mix", "a32", "b32", "ah", "al", "bh", "bl", "dh", "dl", "qh", "ql")
+    names = ("a32", "b32", "ah", "al", "bh", "bl", "dh", "dl", "qh", "ql")
 
     def __init__(self, refs):
         for name, ref in zip(self.names, refs):
@@ -115,16 +122,15 @@
 
     @classmethod
     def shapes(cls, m):
-        return [pltpu.VMEM((m, m), f32)] * 3 + [pltpu.VMEM((m, m), bf16)] * 8
+        return [pltpu.VMEM((m, m), f32)] * 2 + [pltpu.VMEM((m, m), bf16)] * 8
 
 
 def propagators(rows, picked, table, works, wh, wl, first):
     count = rows.shape[1] // 2
-    drift = table.at[table.shape[0] - 1]
     for row, s in zip(picked, works):
         amps = [rows[row, c] for c in range(count)]
         picks = [rows[row, count + c].astype(jnp.int32) for c in range(count)]
-        generator(amps, picks, table, drift, s)
+        generator(amps, picks, table, s)
     for s in works:
         square_step(s)
     for s in works:
@@ -134,29 +140,30 @@
         last_step(s, wh.at[slot], wl.at[slot])
 
 
-def first_kernel(amps, picks, controls, drift, table, wh, wl, mine, *scratch):
-    sems = scratch[-1]
-    kinds, count = controls.shape[0], amps.shape[1]
-    own = [pltpu.make_async_copy(drift, mine.at[count], sems.at[count])]
-    for c in range(count):
-        own.append(pltpu.make_async_copy(controls.at[picks[0, c]], mine.at[c], sems.at[c]))
-    rest = [pltpu.make_async_copy(drift, table.at[kinds], sems.at[count + 1 + kinds])]
+def load_kernel(controls, drift, table, sems):
+    kinds = controls.shape[0]
+
+    def copy(k):
+        return pltpu.make_async_copy(controls.at[k], table.at[k], sems.at[k])
+
+    last = pltpu.make_async_copy(drift, table.at[kinds], sems.at[kinds])
     for k in range(kinds):
-        rest.append(pltpu.make_async_copy(controls.at[k], table.at[k], sems.at[count + 1 + k]))
-    for copy in own + rest:
-        copy.start()
-    for copy in own:
-        copy.wait()
-    s = Work(scratch[:-1])
-    generator([amps[0, c] for c in range(count)], list(range(count)), mine, mine.at[count], s)
-    square_step(s)
-    cube_step(s)
-    last_step(s, wh.at[0], wl.at[0])
-    for copy in rest:
-        copy.wait()
-
-
-def build_kernel(first, rows, table, wh_in, wl_in, wh, wl, *scratch):
+        copy(k).start()
+    last.start()
+
+    def one(k, carry):
+        copy(k).wait()
+        skewed(table.at[k])
+        return carry
+
+    lax.fori_loop(0, kinds, one, 0)
+    last.wait()
+    skewed(table.at[kinds])
+
+
+def build_kernel(first, rows, table, *refs):
+    wh, wl = refs[-2 - 2 * len(Work.names) : -2 * len(Work.names)]
+    scratch = refs[-2 * len(Work.names) :]
     size = len(Work.names)
     slots = rows.shape[0]
     works = [Work(scratch[n * size : (n + 1) * size]) for n in range(len(scratch) // size)]
@@ -233,44 +240,42 @@
         rh[rs, :], rl[rs, :] = split(value)
 
 
-def target_kernel(run, target, out, th, tl, bh, bl):
-    m = target.shape[0]
+def turn_kernel(run, local, target, vh, vl, bh, bl, ph, plo, th, tl):
+    m = run.shape[0]
     for ti in pieces(m, 128):
         bh[ti, :], bl[ti, :] = split(run[ti, :])
         for tj in pieces(m, 128):
             th[ti, tj], tl[ti, tj] = split(target[tj, ti].T)
     for cs in pieces(m, 256):
-        out[:, cs] = dot3(th, tl, bh, bl, cs)
+        vh[:, cs], vl[:, cs] = split(dot3(th, tl, bh, bl, cs))
+    for rs in pieces(m, 32):
+        ph[rs, :], plo[rs, :] = split(local[rs, :])
 
 
 def final_kernel(
-    count, place, picks, run, got, turned, th, tl, local, table, out,
-    ph, plo, bh, bl, vh, vl, x32, kh, kl, uh, ul, g32,
+    count, place, picks, got, turned_h, turned_l, run_h, run_l, local_h, local_l, th, tl, table, out,
+    gh, gl, ph, plo, vh, vl, x32, kh, kl, uh, ul,
 ):
-    m = local.shape[0]
+    m = got.shape[0]
     coarse = place[0]
+    for rs in pieces(m, 32):
+        gh[rs, :], gl[rs, :] = split(got[rs, :])
 
     @pl.when(coarse == 0)
     def _():
-        for rs in pieces(m, 32):
-            uh[rs, :], ul[rs, :] = split(got[rs, :])
-            bh[rs, :], bl[rs, :] = split(run[rs, :])
-            ph[rs, :], plo[rs, :] = split(local[rs, :])
+        for rs in pieces(m, 64):
+            ph[rs, :], plo[rs, :] = local_h[rs, :], local_l[rs, :]
         for cs in pieces(m, 256):
-            vh[:, cs], vl[:, cs] = split(dot3(th, tl, uh, ul, cs))
+            vh[:, cs], vl[:, cs] = split(dot3(th, tl, gh, gl, cs))
         for cs in pieces(m, 256):
-            x32[:, cs] = dot3(vh, vl, bh, bl, cs)
+            x32[:, cs] = dot3(vh, vl, run_h, run_l, cs)
 
     @pl.when(coarse != 0)
     def _():
-        for rs in pieces(m, 32):
-            bh[rs, :], bl[rs, :] = split(got[rs, :])
-            vh[rs, :], vl[rs, :] = split(turned[rs, :])
-            uh[rs, :], ul[rs, :] = split(local[rs, :])
         for cs in pieces(m, 256):
-            x32[:, cs] = dot3(vh, vl, bh, bl, cs)
+            x32[:, cs] = dot3(turned_h, turned_l, gh, gl, cs)
         for cs in pieces(m, 256):
-            ph[:, cs], plo[:, cs] = split(dot3(uh, ul, bh, bl, cs))
+            ph[:, cs], plo[:, cs] = split(dot3(local_h, local_l, gh, gl, cs))
 
     for i, ti in enumerate(pieces(m, 128)):
         for tj in pieces(m, 128)[: i + 1]:
@@ -280,15 +285,21 @@
                 kh[tj, ti], kl[tj, ti] = split(-value.T)
     for cs in pieces(m, 256):
         uh[:, cs], ul[:, cs] = split(dot3(ph, plo, kh, kl, cs))
+    totals = [None] * count
     for cs in pieces(m, 256):
-        g32[:, cs] = (
-            dot_nt(uh[...], ph[cs, :]) + dot_nt(uh[...], plo[cs, :]) + dot_nt(ul[...], ph[cs, :])
-        )
+        for rs in pieces(m, 256):
+            if rs.start < cs.start:
+                continue
+            value = (
+                dot_nt(uh[rs, :], ph[cs, :]) + dot_nt(uh[rs, :], plo[cs, :]) + dot_nt(ul[rs, :], ph[cs, :])
+            )
+            for c in range(count):
+                part = jnp.sum(table[picks[0, c], rs, cs] * value, axis=0, keepdims=True)
+                if rs.start > cs.start:
+                    part = part * 2.0
+                totals[c] = part if totals[c] is None else totals[c] + part
     for c in range(count):
-        total = jnp.zeros((8, m), f32)
-        for rs in pieces(m, 8):
-            total = total + table[picks[0, c], rs, :] * g32[rs, :]
-        out[0, c] = step_scale * jnp.sum(total)
+        out[0, c] = jnp.sum(totals[c])
 
 
 def on_device(amplitudes, control_index, controls, drift_term, target):
@@ -310,49 +321,43 @@
             flops=6 * products * m**3, bytes_accessed=12 * products * m * m, transcendentals=0
         )
 
-    rows = jnp.concatenate([amplitudes, control_index.astype(f32)], axis=1)
-    table = wh = wl = other = None
+    rows = lax.optimization_barrier(jnp.concatenate([amplitudes, control_index.astype(f32)], axis=1))
+    wh = wl = coming = None
     bit = 1
     while bit < order:
         swap = [(i, i ^ bit) for i in range(order)]
+        fresh = rows if bit == 2 else coming
         coming = lax.ppermute(rows, "fine", swap)
         if bit == 1:
-            slots = 8 if short else 1
-            slots = min(slots, order)
-            halves = pltpu.VMEM((slots, m, m), bf16)
-            table, wh, wl = pl.pallas_call(
-                first_kernel,
-                out_shape=(pltpu.VMEM((kinds + 1, m, m), f32), halves, halves),
-                in_specs=[SMEM, SMEM, HBM, HBM],
-                out_specs=(VMEM, VMEM, VMEM),
-                scratch_shapes=[
-                    pltpu.VMEM((count + 1, m, m), f32), *Work.shapes(m),
-                    pltpu.SemaphoreType.DMA((count + kinds + 2,)),
-                ],
-                compiler_params=params(FIRST_MIB),
-                cost_estimate=cost(4),
-                name="first",
-            )(amplitudes, control_index, outside(controls), outside(drift_term))
+            table = pl.pallas_call(
+                load_kernel,
+                out_shape=pltpu.VMEM((kinds + 1, m, m), f32),
+                in_specs=[HBM, HBM],
+                out_specs=VMEM,
+                scratch_shapes=[pltpu.SemaphoreType.DMA((kinds + 1,))],
+                compiler_params=params(LOAD_MIB),
+                cost_estimate=cost(2),
+                name="load",
+            )(outside(controls), outside(drift_term))
         elif short:
-            width = min(2, bit // 2)
+            past = () if wh is None else (inside(wh), inside(wl))
             wh, wl = pl.pallas_call(
-                functools.partial(build_kernel, bit // 2),
-                out_shape=(halves, halves),
-                in_specs=[SMEM, VMEM, VMEM, VMEM],
+                functools.partial(build_kernel, bit - fresh.shape[0]),
+                out_shape=(pltpu.VMEM((order, m, m), bf16),) * 2,
+                in_specs=[SMEM, VMEM] + [VMEM] * len(past),
                 out_specs=(VMEM, VMEM),
-                scratch_shapes=Work.shapes(m) * width,
-                input_output_aliases={2: 0, 3: 1},
+                scratch_shapes=Work.shapes(m) * 2,
+                input_output_aliases={2: 0, 3: 1} if past else {},
                 compiler_params=params(BUILD_MIB),
-                cost_estimate=cost(4 * bit // 2),
+                cost_estimate=cost(4 * fresh.shape[0]),
                 name="build",
-            )(other, *map(inside, (table, wh, wl)))
-        other = coming
-        rows = jnp.concatenate([rows, other], axis=0)
+            )(fresh, inside(table), *past)
+        rows = jnp.concatenate([rows, coming], axis=0)
         bit *= 2
 
     if short:
-        kernel, taken, first = chain_kernel, (other, table, wh, wl), order - other.shape[0]
-        outs, aliases = (square, square, halves, halves), {3: 2, 4: 3}
+        kernel, taken = chain_kernel, (coming, table, wh, wl)
+        outs, aliases = (square, square) + (pltpu.VMEM((order, m, m), bf16),) * 2, {3: 2, 4: 3}
         scratch = [half, half, pltpu.VMEM((2, m, m), f32)]
     else:
         kernel, taken = long_kernel, (rows, table)
@@ -370,29 +375,28 @@
         name="chain",
     )(place, taken[0], *map(inside, taken[1:]))[:2]
     got = lax.ppermute(run, "coarse", [(0, 1), (1, 0)])
-    turned, th, tl = pl.pallas_call(
-        target_kernel,
-        out_shape=(square, half, half),
-        in_specs=[VMEM, VMEM],
-        out_specs=(VMEM, VMEM, VMEM),
-        scratch_shapes=[half] * 2,
+    turned = pl.pallas_call(
+        turn_kernel,
+        out_shape=(half,) * 8,
+        in_specs=[VMEM] * 3,
+        out_specs=(VMEM,) * 8,
         compiler_params=params(TURN_MIB),
         cost_estimate=cost(1),
         name="turn",
-    )(run, target)
+    )(inside(run), inside(local), target)
     return pl.pallas_call(
         functools.partial(final_kernel, count),
         out_shape=jax.ShapeDtypeStruct((1, count), f32),
-        in_specs=[SMEM, SMEM] + [VMEM] * 7,
+        in_specs=[SMEM, SMEM] + [VMEM] * 10,
         out_specs=SMEM,
-        scratch_shapes=[half, half, half, half, half, half, full, half, half, half, half, full],
+        scratch_shapes=[half] * 6 + [full] + [half] * 4,
         compiler_params=params(FINAL_MIB),
         name="final",
-    )(place, control_index, run, got, *map(inside, (turned, th, tl, local, table)))
-
-
-FIRST_MIB = 16
-BUILD_MIB = 16
+    )(place, control_index, got, *map(inside, (*turned, table)))
+
+
+LOAD_MIB = 4
+BUILD_MIB = 14
 CHAIN_MIB = 20
 TURN_MIB = 6
 FINAL_MIB = 12

time: 55.2 us -> 52.8 us (0.957)
  local copies, waits for them, and re-layouts: 1.32 us -> 0.01 us
  Pallas kernels: 42.8 us -> 42 us
    unnamed x8 -> x4, local copies, waits for them, and re-layouts: 1.32 us -> 0.01 us
  transfers between devices with their start and end apart: 4 -> 4, of which waited for: 1 -> 1; matrix products, arithmetic and copies ran while one was open for 0% -> 0% of each run, Pallas kernels for 34% -> 35%
where the time goes in v2:
time: 52.8 us; the launch traced here: 52.2 us
  Pallas kernels  42 us (80%)
  starting transfers between devices  7.37 us (14%)
  other arithmetic  1.48 us (3%)
  waiting for transfers between devices  1.01 us (2%)
    pallas_call x1, Pallas kernels, on_device(): pl.pallas_call(functools.partial(kernel, order), out_shape=outs, in_specs...  18.3 us
    pallas_call x2, Pallas kernels, on_device(): pl.pallas_call(functools.partial(build_kernel, bit - fresh.shape[0]), out...  11.4 us
    ppermute x3, starting transfers between devices, on_device(): coming = lax.ppermute(rows, 'fine', swap)  5.79 us
    pallas_call x1, Pallas kernels, on_device(): pl.pallas_call(load_kernel, out_shape=pltpu.VMEM((kinds + 1, m, m), f32),...  5.65 us
    pallas_call x1, Pallas kernels, on_device(): pl.pallas_call(functools.partial(final_kernel, count), out_shape=jax.Shap...  5.47 us
    ppermute x1, starting transfers between devices, on_device(): got = lax.ppermute(run, 'coarse', [(0, 1), (1, 0)])  1.58 us
    pallas_call x1, Pallas kernels, on_device(): pl.pallas_call(turn_kernel, out_shape=(half,) * 8, in_specs=[VMEM] * 3, o...  1.27 us
  transfers between devices with their start and end apart: 4, of which 1 were waited for; matrix products, arithmetic and copies ran while one was open for 0% of the time, Pallas kernels for 35%

profile of v2, /device:TPU:1, one launch (start us, length us, event | category | flops | bytes accessed | tf_op | source)
XLA Modules:
  0.0 52.2 jit_solution(16386557814790816065)
XLA Ops:
  0.0 0.7 %convert_element_type.3 = f32[1,4]{1,0:T(1,128)S(1)} convert(s32[1,4]{1,0:T(1,128)} %picks.1) | non-fusion elementwise | flops 4 | bytes 32 | tf_op jit(solution)/shard_map/convert_element_type | solution.py:324
  0.7 0.7 %pad_maximum_fusion.2 = f32[1,8]{1,0:T(1,128)S(1)} fusion(f32[1,4]{1,0:T(1,128)S(1)} %convert_element_type.3, f32[1,4]{1,0:T(1,128)} %param.5), kind=kLoop, calls=%fused_computation.3 | loop fusion | flops 8 | bytes 64 | tf_op jit(solution)/shard_map/concatenate | solution.py:324
  1.4 2.1 %collective-permute-start = (f32[1,8]{1,0:T(1,128)S(1)}, f32[1,8]{1,0:T(1,128)S(1)}, u32[]{:S(2)}, u32[]{:S(2)}) collective-permute-start(f32[1,8]{1,0:T(1,128)S(1)} %pad_maximum_fusion.2), channel_id=1, source_target_pairs={{0,1},{1,0},{2,3},{3,2},{4,5},{5,4},{6,7},{7,6},{8,9},{9,8},{10,11... | collective-permute-start | bytes 104 | tf_op jit(solution)/shard_map/ppermute | solution.py:330
  3.4 0.1 pad_add_fusion.place
  3.5 5.6 %load.1.table = f32[9,512,512]{2,1,0:T(8,128)S(1)} custom-call(f32[8,512,512]{2,1,0:T(8,128)} %controls.1, f32[512,512]{1,0:T(8,128)} %drift.1), custom_call_target="tpu_custom_call" | custom-call | flops 1610612736 | bytes 6291456 | tf_op jit(solution)/shard_map/load/pallas_call | solution.py:332
  9.2 0.0 collective-permute-done
  9.2 1.4 %collective-permute-start.1 = (f32[2,8]{1,0:T(2,128)S(1)}, f32[2,8]{1,0:T(2,128)S(1)}, u32[]{:S(2)}, u32[]{:S(2)}) collective-permute-start(f32[2,8]{1,0:T(2,128)S(1)} %pad_maximum_fusion.1.rows), channel_id=1, source_target_pairs={{0,2},{1,3},{2,0},{3,1},{4,6},{5,7},{6,4},{7,5},{8,10},{9,11},{10,... | collective-permute-start | bytes 200 | tf_op jit(solution)/shard_map/ppermute | solution.py:330
  10.6 5.7 %build.2 = (bf16[8,512,512]{2,1,0:T(8,128)(2,1)S(1)}, bf16[8,512,512]{2,1,0:T(8,128)(2,1)S(1)}) custom-call(f32[2,8]{1,0:T(2,128)S(1)} %pad_maximum_fusion.1.rows, f32[9,512,512]{2,1,0:T(8,128)S(1)} %load.1.table), custom_call_target="tpu_custom_call" | custom-call | flops 6442450944 | bytes 25165824 | tf_op jit(solution)/shard_map/build/pallas_call | solution.py:344
  16.3 0.0 collective-permute-done.1.rows
  16.3 2.4 %collective-permute-start.2 = (f32[4,8]{1,0:T(4,128)S(1)}, f32[4,8]{1,0:T(4,128)S(1)}, u32[]{:S(2)}, u32[]{:S(2)}) collective-permute-start(f32[4,8]{1,0:T(4,128)S(1)} %pad_maximum_fusion), channel_id=1, source_target_pairs={{0,4},{1,5},{2,6},{3,7},{4,0},{5,1},{6,2},{7,3},{8,12},{9,13},{10,... | collective-permute-start | bytes 392 | tf_op jit(solution)/shard_map/ppermute | solution.py:330
  18.7 5.7 %build.3 = (bf16[8,512,512]{2,1,0:T(8,128)(2,1)S(1)}, bf16[8,512,512]{2,1,0:T(8,128)(2,1)S(1)}) custom-call(f32[2,8]{1,0:T(2,128)S(1)} %collective-permute-done.1.rows, f32[9,512,512]{2,1,0:T(8,128)S(1)} %load.1.table, bf16[8,512,512]{2,1,0:T(8,128)(2,1)S(1)} %get-tuple-element.19.refs_0_, ...), custom_call_target="tpu_custom_call", output_to_operand_aliasing={{0}: (2, {}), {1}: (3, {})} | custom-call | flops 6442450944 | bytes 25165824 | tf_op jit(solution)/shard_map/build/pallas_call | solution.py:344
  24.4 0.0 collective-permute-done.2.rows
  24.4 0.0 copy-start
  24.4 0.0 copy-start.1
  24.4 18.3 %chain.1 = (f32[512,512]{1,0:T(8,128)S(1)}, f32[512,512]{1,0:T(8,128)S(1)}, bf16[8,512,512]{2,1,0:T(8,128)(2,1)S(1)}, bf16[8,512,512]{2,1,0:T(8,128)(2,1)S(1)}) custom-call(s32[2]{0:T(128)S(1)} %pad_add_fusion.place, f32[4,8]{1,0:T(4,128)S(1)} %collective-permute-done.2.rows, ...), custom_call_target="tpu_custom_call", output_to_operand_aliasing={{2}: (3, {}), {3}: (4, {})} | custom-call | flops 18522046464 | bytes 72351744 | tf_op jit(solution)/shard_map/chain/pallas_call | solution.py:366
  42.7 1.6 %collective-permute-start.3 = (f32[512,512]{1,0:T(8,128)S(1)}, f32[512,512]{1,0:T(8,128)S(1)}, u32[]{:S(2)}, u32[]{:S(2)}) collective-permute-start(f32[512,512]{1,0:T(8,128)S(1)} %get-tuple-element.23.run), channel_id=1, source_target_pairs={{0,8},{8,0},{1,9},{9,1},{2,10},{10,2},{3,11},{11,3},{4,12},{12,4},... | collective-permute-start | bytes 3145736 | tf_op jit(solution)/shard_map/ppermute | solution.py:377
  44.2 0.0 copy-done
  44.2 1.3 %turn.1 = (bf16[512,512]{1,0:T(8,128)(2,1)S(1)}, bf16[512,512]{1,0:T(8,128)(2,1)S(1)}, bf16[512,512]{1,0:T(8,128)(2,1)S(1)}, bf16[512,512]{1,0:T(8,128)(2,1)S(1)...) custom-call(f32[512,512]{1,0:T(8,128)S(1)} %get-tuple-element.23.run, ...), custom_call_target="tpu_custom_call" | custom-call | flops 805306368 | bytes 3145728 | tf_op jit(solution)/shard_map/turn/pallas_call | solution.py:378
  45.5 1.0 %collective-permute-done.3.got = f32[512,512]{1,0:T(8,128)S(1)} collective-permute-done((f32[512,512]{1,0:T(8,128)S(1)}, f32[512,512]{1,0:T(8,128)S(1)}, u32[]{:S(2)}, u32[]{:S(2)}) %collective-permute-start.3) | collective-permute-done | bytes 1048608 | tf_op jit(solution)/shard_map/ppermute | solution.py:377
  46.5 0.0 copy-done.1
  46.5 5.5 %final.1 = f32[1,4]{1,0:T(1,128)} custom-call(s32[2]{0:T(128)S(1)} %pad_add_fusion.place, s32[1,4]{1,0:T(1,128)S(1)} %copy-done.1, f32[512,512]{1,0:T(8,128)S(1)} %collective-permute-done.3.got, bf16[512,512]{1,0:T(8,128)(2,1)S(1)} %get-tuple-element.25.turned_h, bf16[512,512]{1,0:T(8,128)(2,1)S(1)} %get-tuple-element.26.turned_l, ...), custom_call_target="tpu_custom_call" | custom-call | tf_op jit(solution)/shard_map/final/pallas_call | solution.py:387
  (2 shorter events, 0.0 us)
Async XLA Ops:
  1.4 7.8 %collective-permute-start = (f32[1,8]{1,0:T(1,128)S(1)}, f32[1,8]{1,0:T(1,128)S(1)}, u32[]{:S(2)}, u32[]{:S(2)}) collective-permute-start(f32[1,8]{1,0:T(1,128)S(1)} %pad_maximum_fusion.2), channel_id=1, source_target_pairs={{0,1},{1,0},{2,3},{3,2},{4,5},{5,4},{6,7},{7,6},{8,9},{9,8},{10,11... | collective-permute-start | bytes 104 | tf_op jit(solution)/shard_map/ppermute | solution.py:330
  9.2 7.1 %collective-permute-start.1 = (f32[2,8]{1,0:T(2,128)S(1)}, f32[2,8]{1,0:T(2,128)S(1)}, u32[]{:S(2)}, u32[]{:S(2)}) collective-permute-start(f32[2,8]{1,0:T(2,128)S(1)} %pad_maximum_fusion.1.rows), channel_id=1, source_target_pairs={{0,2},{1,3},{2,0},{3,1},{4,6},{5,7},{6,4},{7,5},{8,10},{9,11},{10,... | collective-permute-start | bytes 200 | tf_op jit(solution)/shard_map/ppermute | solution.py:330
  16.3 8.1 %collective-permute-start.2 = (f32[4,8]{1,0:T(4,128)S(1)}, f32[4,8]{1,0:T(4,128)S(1)}, u32[]{:S(2)}, u32[]{:S(2)}) collective-permute-start(f32[4,8]{1,0:T(4,128)S(1)} %pad_maximum_fusion), channel_id=1, source_target_pairs={{0,4},{1,5},{2,6},{3,7},{4,0},{5,1},{6,2},{7,3},{8,12},{9,13},{10,... | collective-permute-start | bytes 392 | tf_op jit(solution)/shard_map/ppermute | solution.py:330
  24.4 19.9 %copy-start = (f32[512,512]{1,0:T(8,128)S(1)}, f32[512,512]{1,0:T(8,128)}, u32[]{:S(2)}) copy-start(f32[512,512]{1,0:T(8,128)} %target.1) | copy-start | bytes 3145732
  24.4 22.1 %copy-start.1 = (s32[1,4]{1,0:T(1,128)S(1)}, s32[1,4]{1,0:T(1,128)}, u32[]{:S(2)}) copy-start(s32[1,4]{1,0:T(1,128)} %picks.1) | copy-start | bytes 52
  42.7 3.9 %collective-permute-start.3 = (f32[512,512]{1,0:T(8,128)S(1)}, f32[512,512]{1,0:T(8,128)S(1)}, u32[]{:S(2)}, u32[]{:S(2)}) collective-permute-start(f32[512,512]{1,0:T(8,128)S(1)} %get-tuple-element.23.run), channel_id=1, source_target_pairs={{0,8},{8,0},{1,9},{9,1},{2,10},{10,2},{3,11},{11,3},{4,12},{12,4},... | collective-permute-start | bytes 3145736 | tf_op jit(solution)/shard_map/ppermute | solution.py:377

commit v3 on v2

--- a/solution.py
+++ b/solution.py
@@ -41,30 +41,27 @@
     )
 
 
+def lower_tiles(m):
+    return [(ti, tj) for i, ti in enumerate(pieces(m, 128)) for tj in pieces(m, 128)[: i + 1]]
+
+
 def skewed(ref):
-    m = ref.shape[0]
-    for i, ti in enumerate(pieces(m, 128)):
-        for tj in pieces(m, 128)[: i + 1]:
-            value = (step_scale * 0.5) * (ref[ti, tj] - ref[tj, ti].T)
-            ref[ti, tj] = value
-            if ti != tj:
-                ref[tj, ti] = -value.T
+    for ti, tj in lower_tiles(ref.shape[0]):
+        ref[ti, tj] = (step_scale * 0.5) * (ref[ti, tj] - ref[tj, ti].T)
 
 
 def generator(amps, picks, table, s):
     kinds = table.shape[0] - 1
-    m = table.shape[1]
-    for i, ti in enumerate(pieces(m, 128)):
-        for tj in pieces(m, 128)[: i + 1]:
-            value = table[kinds, ti, tj]
-            for amp, pick in zip(amps, picks):
-                value = value + amp * table[pick, ti, tj]
-            s.a32[ti, tj] = value
-            s.ah[ti, tj], s.al[ti, tj] = split(value)
-            if ti != tj:
-                back = -value.T
-                s.a32[tj, ti] = back
-                s.ah[tj, ti], s.al[tj, ti] = split(back)
+    for ti, tj in lower_tiles(table.shape[1]):
+        value = table[kinds, ti, tj]
+        for amp, pick in zip(amps, picks):
+            value = value + amp * table[pick, ti, tj]
+        s.a32[ti, tj] = value
+        s.ah[ti, tj], s.al[ti, tj] = split(value)
+        if ti != tj:
+            back = -value.T
+            s.a32[tj, ti] = back
+            s.ah[tj, ti], s.al[tj, ti] = split(back)
 
 
 def mirrored(ah, al, bh, bl, sign, put):
@@ -100,9 +97,20 @@
 
 
 def last_step(s, wh, wl):
-    for cs in pieces(s.ah.shape[0], 256):
+    m = s.ah.shape[0]
+    for cs in pieces(m, 256):
         value = dot3(s.dh, s.dl, s.qh, s.ql, cs) + s.a32[:, cs]
-        wh[:, cs], wl[:, cs] = split(value)
+        for rs in pieces(m, 256):
+            part = value[rs, :]
+            if rs == cs:
+                part = part + unit(part.shape)
+            wh[rs, cs], wl[rs, cs] = split(part)
+
+
+def unit(shape):
+    return (
+        lax.broadcasted_iota(jnp.int32, shape, 0) == lax.broadcasted_iota(jnp.int32, shape, 1)
+    ).astype(f32)
 
 
 def inside(x):
@@ -151,27 +159,33 @@
         copy(k).start()
     last.start()
 
-    def one(k, carry):
-        copy(k).wait()
-        skewed(table.at[k])
-        return carry
-
-    lax.fori_loop(0, kinds, one, 0)
-    last.wait()
-    skewed(table.at[kinds])
+    waits = [copy(k) for k in range(kinds)] + [last]
+    for at in range(0, kinds + 1, 3):
+        group = range(at, min(at + 3, kinds + 1))
+        for k in group:
+            waits[k].wait()
+        for k in group:
+            skewed(table.at[k])
 
 
 def build_kernel(first, rows, table, *refs):
-    wh, wl = refs[-2 - 2 * len(Work.names) : -2 * len(Work.names)]
-    scratch = refs[-2 * len(Work.names) :]
     size = len(Work.names)
-    slots = rows.shape[0]
-    works = [Work(scratch[n * size : (n + 1) * size]) for n in range(len(scratch) // size)]
-    for n in range(0, slots, len(works)):
-        propagators(rows, range(n, n + len(works)), table, works, wh, wl, first)
-
-
-def chain_kernel(order, place, rows, table, wh_in, wl_in, run, local, wh, wl, rh, rl, both, *scratch):
+    width = rows.shape[0]
+    wh, wl = refs[-2 - width * size : -width * size]
+    scratch = refs[-width * size :]
+    works = [Work(scratch[n * size : (n + 1) * size]) for n in range(width)]
+    propagators(rows, range(width), table, works, wh, wl, first)
+
+
+def join(run, wh, wl, rh, rl):
+    for cs in pieces(rh.shape[0], 256):
+        value = dot3(wh, wl, rh, rl, cs)
+        if run is not None:
+            run[:, cs] = value
+        yield cs, split(value)
+
+
+def chain_kernel(order, place, rows, table, wh_in, wl_in, run, lh, ll, wh, wl, rh, rl, bh, bl, *scratch):
     size = len(Work.names)
     works = [Work(scratch[n * size : (n + 1) * size]) for n in range(2)]
     m = run.shape[0]
@@ -183,64 +197,48 @@
         return carry
 
     lax.fori_loop(0, rows.shape[0] // 2, pair, 0)
-    start_product(fine, wh.at[fine], wl.at[fine], run, rh, rl)
-    for rs in pieces(m, 32):
-        both[0, rs, :] = run[rs, :]
+    for rs in pieces(m, 64):
+        high, low = wh[fine, rs, :], wl[fine, rs, :]
+        rh[rs, :], rl[rs, :] = high, low
+        bh[0, rs, :], bl[0, rs, :] = high, low
     for step in range(1, order):
         slot = step ^ fine
         side = jnp.where(step <= fine, 0, 1)
-        for cs in pieces(m, 256):
-            value = dot3(wh.at[slot], wl.at[slot], rh, rl, cs) + run[:, cs]
-            run[:, cs] = value
-            both[side, :, cs] = value
-            rh[:, cs], rl[:, cs] = split(value)
-    for rs in pieces(m, 32):
-        local[rs, :] = both[0, rs, :]
-
-
-def long_kernel(order, place, rows, table, run, local, wh, wl, rh, rl, *scratch):
+        for cs, (high, low) in join(run if step == order - 1 else None, wh.at[slot], wl.at[slot], rh, rl):
+            rh[:, cs], rl[:, cs] = high, low
+            bh[side, :, cs], bl[side, :, cs] = high, low
+    for rs in pieces(m, 64):
+        lh[rs, :], ll[rs, :] = bh[0, rs, :], bl[0, rs, :]
+
+
+def long_kernel(order, place, rows, table, run, lh, ll, wh, wl, rh, rl, *scratch):
     size = len(Work.names)
     works = [Work(scratch[n * size : (n + 1) * size]) for n in range(2)]
     m = run.shape[0]
     fine = place[1]
-    for rs in pieces(m, 32):
-        value = unit(rs, m)
-        run[rs, :] = value
-        rh[rs, :], rl[rs, :] = split(value)
+    for rs in pieces(m, 256):
+        for cs in pieces(m, 256):
+            shape = (rs.stop - rs.start, cs.stop - cs.start)
+            rh[rs, cs], rl[rs, cs] = split(unit(shape) if rs == cs else jnp.zeros(shape, f32))
 
     def pair(n, carry):
         steps = [2 * n, 2 * n + 1]
         propagators(rows, [step ^ fine for step in steps], table, works, wh, wl, None)
         for k, step in enumerate(steps):
-            for cs in pieces(m, 256):
-                value = dot3(wh.at[k], wl.at[k], rh, rl, cs) + run[:, cs]
-                run[:, cs] = value
-                rh[:, cs], rl[:, cs] = split(value)
+            for cs, (high, low) in join(run, wh.at[k], wl.at[k], rh, rl):
+                rh[:, cs], rl[:, cs] = high, low
 
             @pl.when(step == fine)
             def _():
-                for rs in pieces(m, 32):
-                    local[rs, :] = run[rs, :]
+                for rs in pieces(m, 64):
+                    lh[rs, :], ll[rs, :] = rh[rs, :], rl[rs, :]
 
         return carry
 
     lax.fori_loop(0, order // 2, pair, 0)
 
 
-def unit(rs, m):
-    at = lax.broadcasted_iota(jnp.int32, (rs.stop - rs.start, m), 0) + rs.start
-    return (at == lax.broadcasted_iota(jnp.int32, (rs.stop - rs.start, m), 1)).astype(f32)
-
-
-def start_product(fine, wh, wl, run, rh, rl):
-    m = run.shape[0]
-    for rs in pieces(m, 32):
-        value = wh[rs, :].astype(f32) + wl[rs, :].astype(f32) + unit(rs, m)
-        run[rs, :] = value
-        rh[rs, :], rl[rs, :] = split(value)
-
-
-def turn_kernel(run, local, target, vh, vl, bh, bl, ph, plo, th, tl):
+def turn_kernel(run, target, vh, vl, bh, bl, th, tl):
     m = run.shape[0]
     for ti in pieces(m, 128):
         bh[ti, :], bl[ti, :] = split(run[ti, :])
@@ -248,8 +246,6 @@
             th[ti, tj], tl[ti, tj] = split(target[tj, ti].T)
     for cs in pieces(m, 256):
         vh[:, cs], vl[:, cs] = split(dot3(th, tl, bh, bl, cs))
-    for rs in pieces(m, 32):
-        ph[rs, :], plo[rs, :] = split(local[rs, :])
 
 
 def final_kernel(
@@ -285,7 +281,7 @@
                 kh[tj, ti], kl[tj, ti] = split(-value.T)
     for cs in pieces(m, 256):
         uh[:, cs], ul[:, cs] = split(dot3(ph, plo, kh, kl, cs))
-    totals = [None] * count
+    totals = [jnp.zeros((8, 128), f32)] * count
     for cs in pieces(m, 256):
         for rs in pieces(m, 256):
             if rs.start < cs.start:
@@ -293,11 +289,16 @@
             value = (
                 dot_nt(uh[rs, :], ph[cs, :]) + dot_nt(uh[rs, :], plo[cs, :]) + dot_nt(ul[rs, :], ph[cs, :])
             )
-            for c in range(count):
-                part = jnp.sum(table[picks[0, c], rs, cs] * value, axis=0, keepdims=True)
-                if rs.start > cs.start:
-                    part = part * 2.0
-                totals[c] = part if totals[c] is None else totals[c] + part
+            for ti, tj in lower_tiles(m):
+                if not (rs.start <= ti.start < rs.stop and cs.start <= tj.start < cs.stop):
+                    continue
+                tile = value[ti.start - rs.start : ti.stop - rs.start, tj.start - cs.start : tj.stop - cs.start]
+                if ti != tj:
+                    tile = tile + tile
+                for c in range(count):
+                    part = table[picks[0, c], ti, tj] * tile
+                    for at in range(0, part.shape[0], 8):
+                        totals[c] = totals[c] + part[at : at + 8, :]
     for c in range(count):
         out[0, c] = jnp.sum(totals[c])
 
@@ -321,14 +322,20 @@
             flops=6 * products * m**3, bytes_accessed=12 * products * m * m, transcendentals=0
         )
 
-    rows = lax.optimization_barrier(jnp.concatenate([amplitudes, control_index.astype(f32)], axis=1))
-    wh = wl = coming = None
+    wh = wl = coming = rows = None
     bit = 1
     while bit < order:
         swap = [(i, i ^ bit) for i in range(order)]
         fresh = rows if bit == 2 else coming
-        coming = lax.ppermute(rows, "fine", swap)
-        if bit == 1:
+        if bit > 1:
+            coming = lax.ppermute(rows, "fine", swap)
+            rows_next = (rows, coming)
+        else:
+            both = lax.ppermute((amplitudes, control_index), "fine", swap)
+            rows_next = [
+                jnp.concatenate([amps, picks.astype(f32)], axis=1)
+                for amps, picks in ((amplitudes, control_index), both)
+            ]
             table = pl.pallas_call(
                 load_kernel,
                 out_shape=pltpu.VMEM((kinds + 1, m, m), f32),
@@ -339,7 +346,7 @@
                 cost_estimate=cost(2),
                 name="load",
             )(outside(controls), outside(drift_term))
-        elif short:
+        if bit > 1 and short:
             past = () if wh is None else (inside(wh), inside(wl))
             wh, wl = pl.pallas_call(
                 functools.partial(build_kernel, bit - fresh.shape[0]),
@@ -352,18 +359,18 @@
                 cost_estimate=cost(4 * fresh.shape[0]),
                 name="build",
             )(fresh, inside(table), *past)
-        rows = jnp.concatenate([rows, coming], axis=0)
+        rows = jnp.concatenate(rows_next, axis=0)
         bit *= 2
 
     if short:
         kernel, taken = chain_kernel, (coming, table, wh, wl)
-        outs, aliases = (square, square) + (pltpu.VMEM((order, m, m), bf16),) * 2, {3: 2, 4: 3}
-        scratch = [half, half, pltpu.VMEM((2, m, m), f32)]
+        outs, aliases = (square, half, half) + (pltpu.VMEM((order, m, m), bf16),) * 2, {3: 3, 4: 4}
+        scratch = [half, half] + [pltpu.VMEM((2, m, m), bf16)] * 2
     else:
         kernel, taken = long_kernel, (rows, table)
-        outs, aliases = (square, square), {}
+        outs, aliases = (square, half, half), {}
         scratch = [pltpu.VMEM((2, m, m), bf16), pltpu.VMEM((2, m, m), bf16), half, half]
-    run, local = pl.pallas_call(
+    run, lh, ll = pl.pallas_call(
         functools.partial(kernel, order),
         out_shape=outs,
         in_specs=[SMEM, SMEM] + [VMEM] * (len(taken) - 1),
@@ -373,17 +380,17 @@
         compiler_params=params(CHAIN_MIB),
         cost_estimate=cost(23),
         name="chain",
-    )(place, taken[0], *map(inside, taken[1:]))[:2]
+    )(place, taken[0], *map(inside, taken[1:]))[:3]
     got = lax.ppermute(run, "coarse", [(0, 1), (1, 0)])
     turned = pl.pallas_call(
         turn_kernel,
-        out_shape=(half,) * 8,
-        in_specs=[VMEM] * 3,
-        out_specs=(VMEM,) * 8,
+        out_shape=(half,) * 6,
+        in_specs=[VMEM] * 2,
+        out_specs=(VMEM,) * 6,
         compiler_params=params(TURN_MIB),
         cost_estimate=cost(1),
         name="turn",
-    )(inside(run), inside(local), target)
+    )(inside(run), target)
     return pl.pallas_call(
         functools.partial(final_kernel, count),
         out_shape=jax.ShapeDtypeStruct((1, count), f32),
@@ -392,7 +399,7 @@
         scratch_shapes=[half] * 6 + [full] + [half] * 4,
         compiler_params=params(FINAL_MIB),
         name="final",
-    )(place, control_index, got, *map(inside, (*turned, table)))
+    )(place, control_index, got, *map(inside, (*turned[:4], lh, ll, *turned[4:], table)))
 
 
 LOAD_MIB = 4

time: 52.8 us -> 50.6 us (0.958)
  Pallas kernels: 42 us -> 40 us
  other arithmetic: 1.48 us -> 0.93 us
    ppermute x0 -> x2, starting transfers between devices: none -> 2.08 us  [on_device(): both = lax.ppermute((amplitudes, control_index), 'fine', swap)]
    ppermute x3 -> x2, starting transfers between devices: 5.79 us -> 3.82 us  [on_device(): coming = lax.ppermute(rows, 'fine', swap)]
    pallas_call x1, Pallas kernels: 5.65 us -> 4.36 us  [on_device(): pl.pallas_call(load_kernel, out_shape=pltpu.VMEM((kinds + 1, m, m), f32),...]
    pallas_call x1, Pallas kernels: 18.3 us -> 17.7 us  [on_device(): pl.pallas_call(functools.partial(kernel, order), out_shape=outs, in_specs...]
    concatenate x3 -> x2, other arithmetic: 0.75 us -> 0.16 us  [on_device(): rows = jnp.concatenate(rows_next, axis=0)]
  transfers between devices with their start and end apart: 4 -> 5, of which waited for: 1 -> 1; matrix products, arithmetic and copies ran while one was open for 0% -> 2% of each run, Pallas kernels for 35% -> 34%
where the time goes in v3:
time: 50.6 us; the launch traced here: 50.1 us
  Pallas kernels  40 us (79%)
  starting transfers between devices  7.77 us (15%)
  waiting for transfers between devices  1.13 us (2%)
  other arithmetic  0.93 us (2%)
    pallas_call x1, Pallas kernels, on_device(): pl.pallas_call(functools.partial(kernel, order), out_shape=outs, in_specs...  17.7 us
    pallas_call x2, Pallas kernels, on_device(): pl.pallas_call(functools.partial(build_kernel, bit - fresh.shape[0]), out...  11.5 us
    pallas_call x1, Pallas kernels, on_device(): pl.pallas_call(functools.partial(final_kernel, count), out_shape=jax.Shap...  5.29 us
    pallas_call x1, Pallas kernels, on_device(): pl.pallas_call(load_kernel, out_shape=pltpu.VMEM((kinds + 1, m, m), f32),...  4.36 us
    ppermute x2, starting transfers between devices, on_device(): coming = lax.ppermute(rows, 'fine', swap)  3.82 us
    ppermute x2, starting transfers between devices, on_device(): both = lax.ppermute((amplitudes, control_index), 'fine', swap)  2.08 us
    ppermute x1, starting transfers between devices, on_device(): got = lax.ppermute(run, 'coarse', [(0, 1), (1, 0)])  1.87 us
    pallas_call x1, Pallas kernels, on_device(): pl.pallas_call(turn_kernel, out_shape=(half,) * 6, in_specs=[VMEM] * 2, o...  1.16 us
  transfers between devices with their start and end apart: 5, of which 1 were waited for; matrix products, arithmetic and copies ran while one was open for 2% of the time, Pallas kernels for 34%

profile of v3, /device:TPU:1, one launch (start us, length us, event | category | flops | bytes accessed | tf_op | source)
XLA Modules:
  0.0 50.1 jit_solution(1305841482143649152)
XLA Ops:
  0.0 2.1 %collective-permute-start = (f32[1,4]{1,0:T(1,128)}, f32[1,4]{1,0:T(1,128)S(1)}, u32[]{:S(2)}, u32[]{:S(2)}) collective-permute-start(f32[1,4]{1,0:T(1,128)} %param.5), channel_id=1, source_target_pairs={{0,1},{1,0},{2,3},{3,2},{4,5},{5,4},{6,7},{7,6},{8,9},{9,8},{10,11... | collective-permute-start | bytes 56 | tf_op jit(solution)/shard_map/ppermute | solution.py:334
  2.1 0.0 collective-permute-start.1
  2.1 0.7 %convert_element_type.6 = f32[1,4]{1,0:T(1,128)S(1)} convert(s32[1,4]{1,0:T(1,128)} %picks.1) | non-fusion elementwise | flops 4 | bytes 32 | tf_op jit(solution)/shard_map/convert_element_type | solution.py:336
  2.8 0.1 pad_add_fusion.place
  2.8 4.4 %load.1.table = f32[9,512,512]{2,1,0:T(8,128)S(1)} custom-call(f32[8,512,512]{2,1,0:T(8,128)} %controls.1, f32[512,512]{1,0:T(8,128)} %drift.1), custom_call_target="tpu_custom_call" | custom-call | flops 1610612736 | bytes 6291456 | tf_op jit(solution)/shard_map/load/pallas_call | solution.py:339
  7.2 0.0 collective-permute-done.1
  7.2 0.0 collective-permute-done
  7.3 0.0 copy-done.2
  7.3 0.1 maximum_maximum_fusion.rows
  7.3 1.5 %collective-permute-start.2 = (f32[2,8]{1,0:T(2,128)S(1)}, f32[2,8]{1,0:T(2,128)S(1)}, u32[]{:S(2)}, u32[]{:S(2)}) collective-permute-start(f32[2,8]{1,0:T(2,128)S(1)} %maximum_maximum_fusion.rows), channel_id=1, source_target_pairs={{0,2},{1,3},{2,0},{3,1},{4,6},{5,7},{6,4},{7,5},{8,10},{9,11},{10,... | collective-permute-start | bytes 200 | tf_op jit(solution)/shard_map/ppermute | solution.py:331
  8.8 5.8 %build.2 = (bf16[8,512,512]{2,1,0:T(8,128)(2,1)S(1)}, bf16[8,512,512]{2,1,0:T(8,128)(2,1)S(1)}) custom-call(f32[2,8]{1,0:T(2,128)S(1)} %maximum_maximum_fusion.rows, f32[9,512,512]{2,1,0:T(8,128)S(1)} %load.1.table), custom_call_target="tpu_custom_call" | custom-call | flops 6442450944 | bytes 25165824 | tf_op jit(solution)/shard_map/build/pallas_call | solution.py:351
  14.6 0.0 collective-permute-done.2.rows
  14.6 0.1 pad_maximum_fusion
  14.7 2.3 %collective-permute-start.3 = (f32[4,8]{1,0:T(4,128)S(1)}, f32[4,8]{1,0:T(4,128)S(1)}, u32[]{:S(2)}, u32[]{:S(2)}) collective-permute-start(f32[4,8]{1,0:T(4,128)S(1)} %pad_maximum_fusion), channel_id=1, source_target_pairs={{0,4},{1,5},{2,6},{3,7},{4,0},{5,1},{6,2},{7,3},{8,12},{9,13},{10,... | collective-permute-start | bytes 392 | tf_op jit(solution)/shard_map/ppermute | solution.py:331
  17.0 5.7 %build.3 = (bf16[8,512,512]{2,1,0:T(8,128)(2,1)S(1)}, bf16[8,512,512]{2,1,0:T(8,128)(2,1)S(1)}) custom-call(f32[2,8]{1,0:T(2,128)S(1)} %collective-permute-done.2.rows, f32[9,512,512]{2,1,0:T(8,128)S(1)} %load.1.table, bf16[8,512,512]{2,1,0:T(8,128)(2,1)S(1)} %get-tuple-element.18.refs_0_, ...), custom_call_target="tpu_custom_call", output_to_operand_aliasing={{0}: (2, {}), {1}: (3, {})} | custom-call | flops 6442450944 | bytes 25165824 | tf_op jit(solution)/shard_map/build/pallas_call | solution.py:351
  22.8 0.0 collective-permute-done.3.rows
  22.8 0.0 copy-start.1
  22.8 0.0 copy-start
  22.8 17.7 %chain.1 = (f32[512,512]{1,0:T(8,128)S(1)}, bf16[512,512]{1,0:T(8,128)(2,1)S(1)}, bf16[512,512]{1,0:T(8,128)(2,1)S(1)}, bf16[8,512,512]{2,1,0:T(8,128)(2,1)S(1)}, bf16[8,512,512]{2,1,0:T(8,128)(2,1)S(1)}) custom-call(s32[2]{0:T(128)S(1)} %pad_add_fusion.place, f32[4,8]{1,0:T(4,128)S(1)} %collective-permute-done.3.rows, ...), custom_call_target="tpu_custom_call", output_to_operand_aliasing={{3}: (3, {}), {4}: (4, {})} | custom-call | flops 18522046464 | bytes 72351744 | tf_op jit(solution)/shard_map/chain/pallas_call | solution.py:373
  40.5 1.9 %collective-permute-start.4 = (f32[512,512]{1,0:T(8,128)S(1)}, f32[512,512]{1,0:T(8,128)S(1)}, u32[]{:S(2)}, u32[]{:S(2)}) collective-permute-start(f32[512,512]{1,0:T(8,128)S(1)} %get-tuple-element.22.run), channel_id=1, source_target_pairs={{0,8},{8,0},{1,9},{9,1},{2,10},{10,2},{3,11},{11,3},{4,12},{12,4},... | collective-permute-start | bytes 3145736 | tf_op jit(solution)/shard_map/ppermute | solution.py:384
  42.3 0.0 copy-done.1
  42.3 1.2 %turn.1 = (bf16[512,512]{1,0:T(8,128)(2,1)S(1)}, bf16[512,512]{1,0:T(8,128)(2,1)S(1)}, bf16[512,512]{1,0:T(8,128)(2,1)S(1)}, bf16[512,512]{1,0:T(8,128)(2,1)S(1)...) custom-call(f32[512,512]{1,0:T(8,128)S(1)} %get-tuple-element.22.run, f32[512,512]{1,0:T(8,128)S(1)} %copy-done.1), custom_call_target="tpu_custom_call" | custom-call | flops 805306368 | bytes 3145728 | tf_op jit(solution)/shard_map/turn/pallas_call | solution.py:385
  43.5 1.1 %collective-permute-done.4.got = f32[512,512]{1,0:T(8,128)S(1)} collective-permute-done((f32[512,512]{1,0:T(8,128)S(1)}, f32[512,512]{1,0:T(8,128)S(1)}, u32[]{:S(2)}, u32[]{:S(2)}) %collective-permute-start.4) | collective-permute-done | bytes 1048608 | tf_op jit(solution)/shard_map/ppermute | solution.py:384
  44.6 5.3 %final.1 = f32[1,4]{1,0:T(1,128)} custom-call(s32[2]{0:T(128)S(1)} %pad_add_fusion.place, s32[1,4]{1,0:T(1,128)S(1)} %copy-done, f32[512,512]{1,0:T(8,128)S(1)} %collective-permute-done.4.got, bf16[512,512]{1,0:T(8,128)(2,1)S(1)} %get-tuple-element.23.turned_h, bf16[512,512]{1,0:T(8,128)(2,1)S(1)} %get-tuple-element.24.turned_l, ...), custom_call_target="tpu_custom_call" | custom-call | tf_op jit(solution)/shard_map/final/pallas_call | solution.py:394
  (3 shorter events, 0.0 us)
Async XLA Ops:
  0.0 7.2 %collective-permute-start = (f32[1,4]{1,0:T(1,128)}, f32[1,4]{1,0:T(1,128)S(1)}, u32[]{:S(2)}, u32[]{:S(2)}) collective-permute-start(f32[1,4]{1,0:T(1,128)} %param.5), channel_id=1, source_target_pairs={{0,1},{1,0},{2,3},{3,2},{4,5},{5,4},{6,7},{7,6},{8,9},{9,8},{10,11... | collective-permute-start | bytes 56 | tf_op jit(solution)/shard_map/ppermute | solution.py:334
  2.1 5.2 %collective-permute-start.1 = (s32[1,4]{1,0:T(1,128)}, s32[1,4]{1,0:T(1,128)S(1)}, u32[]{:S(2)}, u32[]{:S(2)}) collective-permute-start(s32[1,4]{1,0:T(1,128)} %picks.1), channel_id=1, source_target_pairs={{0,1},{1,0},{2,3},{3,2},{4,5},{5,4},{6,7},{7,6},{8,9},{9,8},{10,11... | collective-permute-start | bytes 56 | tf_op jit(solution)/shard_map/ppermute | solution.py:334
  2.8 4.4 %copy-start.2 = (f32[1,4]{1,0:T(1,128)S(1)}, f32[1,4]{1,0:T(1,128)}, u32[]{:S(2)}) copy-start(f32[1,4]{1,0:T(1,128)} %param.5) | copy-start | bytes 52
  7.3 7.3 %collective-permute-start.2 = (f32[2,8]{1,0:T(2,128)S(1)}, f32[2,8]{1,0:T(2,128)S(1)}, u32[]{:S(2)}, u32[]{:S(2)}) collective-permute-start(f32[2,8]{1,0:T(2,128)S(1)} %maximum_maximum_fusion.rows), channel_id=1, source_target_pairs={{0,2},{1,3},{2,0},{3,1},{4,6},{5,7},{6,4},{7,5},{8,10},{9,11},{10,... | collective-permute-start | bytes 200 | tf_op jit(solution)/shard_map/ppermute | solution.py:331
  14.7 8.1 %collective-permute-start.3 = (f32[4,8]{1,0:T(4,128)S(1)}, f32[4,8]{1,0:T(4,128)S(1)}, u32[]{:S(2)}, u32[]{:S(2)}) collective-permute-start(f32[4,8]{1,0:T(4,128)S(1)} %pad_maximum_fusion), channel_id=1, source_target_pairs={{0,4},{1,5},{2,6},{3,7},{4,0},{5,1},{6,2},{7,3},{8,12},{9,13},{10,... | collective-permute-start | bytes 392 | tf_op jit(solution)/shard_map/ppermute | solution.py:331
  22.8 19.6 %copy-start.1 = (f32[512,512]{1,0:T(8,128)S(1)}, f32[512,512]{1,0:T(8,128)}, u32[]{:S(2)}) copy-start(f32[512,512]{1,0:T(8,128)} %target.1) | copy-start | bytes 3145732
  22.8 21.8 %copy-start = (s32[1,4]{1,0:T(1,128)S(1)}, s32[1,4]{1,0:T(1,128)}, u32[]{:S(2)}) copy-start(s32[1,4]{1,0:T(1,128)} %picks.1) | copy-start | bytes 52
  40.5 4.2 %collective-permute-start.4 = (f32[512,512]{1,0:T(8,128)S(1)}, f32[512,512]{1,0:T(8,128)S(1)}, u32[]{:S(2)}, u32[]{:S(2)}) collective-permute-start(f32[512,512]{1,0:T(8,128)S(1)} %get-tuple-element.22.run), channel_id=1, source_target_pairs={{0,8},{8,0},{1,9},{9,1},{2,10},{10,2},{3,11},{11,3},{4,12},{12,4},... | collective-permute-start | bytes 3145736 | tf_op jit(solution)/shard_map/ppermute | solution.py:384

commit v4 on v3

--- a/solution.py
+++ b/solution.py
@@ -133,18 +133,15 @@
         return [pltpu.VMEM((m, m), f32)] * 2 + [pltpu.VMEM((m, m), bf16)] * 8
 
 
-def propagators(rows, picked, table, works, wh, wl, first):
-    count = rows.shape[1] // 2
+def propagators(amps, picks, picked, works, table, wh, wl, slots):
+    count = amps.shape[1]
     for row, s in zip(picked, works):
-        amps = [rows[row, c] for c in range(count)]
-        picks = [rows[row, count + c].astype(jnp.int32) for c in range(count)]
-        generator(amps, picks, table, s)
+        generator([amps[row, c] for c in range(count)], [picks[row, c] for c in range(count)], table, s)
     for s in works:
         square_step(s)
     for s in works:
         cube_step(s)
-    for k, (row, s) in enumerate(zip(picked, works)):
-        slot = k if first is None else first + row
+    for slot, s in zip(slots, works):
         last_step(s, wh.at[slot], wl.at[slot])
 
 
@@ -168,52 +165,65 @@
             skewed(table.at[k])
 
 
-def build_kernel(first, rows, table, *refs):
+def works_of(scratch):
     size = len(Work.names)
-    width = rows.shape[0]
+    return [Work(scratch[at : at + size]) for at in range(0, len(scratch), size)]
+
+
+def build_kernel(first, amps, picks, table, *refs):
+    size = len(Work.names)
+    width = amps.shape[0]
     wh, wl = refs[-2 - width * size : -width * size]
-    scratch = refs[-width * size :]
-    works = [Work(scratch[n * size : (n + 1) * size]) for n in range(width)]
-    propagators(rows, range(width), table, works, wh, wl, first)
-
-
-def join(run, wh, wl, rh, rl):
-    for cs in pieces(rh.shape[0], 256):
-        value = dot3(wh, wl, rh, rl, cs)
-        if run is not None:
-            run[:, cs] = value
-        yield cs, split(value)
-
-
-def chain_kernel(order, place, rows, table, wh_in, wl_in, run, lh, ll, wh, wl, rh, rl, bh, bl, *scratch):
-    size = len(Work.names)
-    works = [Work(scratch[n * size : (n + 1) * size]) for n in range(2)]
-    m = run.shape[0]
+    slots = [first + n for n in range(width)]
+    propagators(amps, picks, range(width), works_of(refs[-width * size :]), table, wh, wl, slots)
+
+
+def multiply(ah, al, bh, bl):
+    for cs in pieces(ah.shape[0], 256):
+        yield cs, dot3(ah, al, bh, bl, cs)
+
+
+def chain_kernel(
+    place, amps, picks, table, early_h, early_l, run, lh, ll, oh, ol,
+    wh, wl, th, tl, qh, ql, bh, bl, *scratch
+):
+    half, m = early_h.shape[:2]
     fine = place[1]
-    first = order - rows.shape[0]
-
-    def pair(n, carry):
-        propagators(rows, [2 * n, 2 * n + 1], table, works, wh, wl, first)
-        return carry
-
-    lax.fori_loop(0, rows.shape[0] // 2, pair, 0)
+    inner = fine & (half - 1)
+    upper = jnp.where(fine < half, 1, 0)
+    propagators(amps, picks, range(half), works_of(scratch), table, wh, wl, range(half))
     for rs in pieces(m, 64):
-        high, low = wh[fine, rs, :], wl[fine, rs, :]
-        rh[rs, :], rl[rs, :] = high, low
+        high, low = early_h[inner, rs, :], early_l[inner, rs, :]
+        qh[0, rs, :], ql[0, rs, :] = high, low
         bh[0, rs, :], bl[0, rs, :] = high, low
-    for step in range(1, order):
-        slot = step ^ fine
-        side = jnp.where(step <= fine, 0, 1)
-        for cs, (high, low) in join(run if step == order - 1 else None, wh.at[slot], wl.at[slot], rh, rl):
-            rh[:, cs], rl[:, cs] = high, low
+    for step in range(1, half):
+        slot = step ^ inner
+        side = jnp.where(step <= inner, 0, 1)
+        for cs, value in multiply(early_h.at[slot], early_l.at[slot], qh.at[0], ql.at[0]):
+            high, low = split(value)
+            qh[0, :, cs], ql[0, :, cs] = high, low
             bh[side, :, cs], bl[side, :, cs] = high, low
     for rs in pieces(m, 64):
         lh[rs, :], ll[rs, :] = bh[0, rs, :], bl[0, rs, :]
-
-
-def long_kernel(order, place, rows, table, run, lh, ll, wh, wl, rh, rl, *scratch):
-    size = len(Work.names)
-    works = [Work(scratch[n * size : (n + 1) * size]) for n in range(2)]
+    level = [(wh.at[step ^ inner], wl.at[step ^ inner]) for step in range(half)]
+    free = 0
+    while len(level) > 1:
+        above = []
+        for n in range(0, len(level), 2):
+            goal = (qh.at[1], ql.at[1]) if len(level) == 2 else (th.at[free], tl.at[free])
+            free += 1
+            for cs, value in multiply(*level[n + 1], *level[n]):
+                goal[0][:, cs], goal[1][:, cs] = split(value)
+            above.append(goal)
+        level = above
+    for cs, value in multiply(qh.at[upper], ql.at[upper], qh.at[1 - upper], ql.at[1 - upper]):
+        run[:, cs] = value
+    for rs in pieces(m, 64):
+        oh[rs, :], ol[rs, :] = qh[1, rs, :], ql[1, rs, :]
+
+
+def long_kernel(order, place, amps, picks, table, run, lh, ll, wh, wl, rh, rl, *scratch):
+    works = works_of(scratch)
     m = run.shape[0]
     fine = place[1]
     for rs in pieces(m, 256):
@@ -223,10 +233,11 @@
 
     def pair(n, carry):
         steps = [2 * n, 2 * n + 1]
-        propagators(rows, [step ^ fine for step in steps], table, works, wh, wl, None)
+        propagators(amps, picks, [step ^ fine for step in steps], works, table, wh, wl, range(2))
         for k, step in enumerate(steps):
-            for cs, (high, low) in join(run, wh.at[k], wl.at[k], rh, rl):
-                rh[:, cs], rl[:, cs] = high, low
+            for cs, value in multiply(wh.at[k], wl.at[k], rh, rl):
+                run[:, cs] = value
+                rh[:, cs], rl[:, cs] = split(value)
 
             @pl.when(step == fine)
             def _():
@@ -238,14 +249,29 @@
     lax.fori_loop(0, order // 2, pair, 0)
 
 
-def turn_kernel(run, target, vh, vl, bh, bl, th, tl):
+def turn_kernel(half, place, run, target, lh, ll, *refs):
+    below = refs[: len(refs) - 8]
+    vh, vl, bh, bl, ph, plo, th, tl = refs[len(refs) - 8 :]
     m = run.shape[0]
     for ti in pieces(m, 128):
         bh[ti, :], bl[ti, :] = split(run[ti, :])
         for tj in pieces(m, 128):
             th[ti, tj], tl[ti, tj] = split(target[tj, ti].T)
-    for cs in pieces(m, 256):
-        vh[:, cs], vl[:, cs] = split(dot3(th, tl, bh, bl, cs))
+    for cs, value in multiply(th, tl, bh, bl):
+        vh[:, cs], vl[:, cs] = split(value)
+    first = True if not below else place[1] < half
+
+    @pl.when(first)
+    def _():
+        for rs in pieces(m, 64):
+            ph[rs, :], plo[rs, :] = lh[rs, :], ll[rs, :]
+
+    if below:
+
+        @pl.when(place[1] >= half)
+        def _():
+            for cs, value in multiply(lh, ll, *below):
+                ph[:, cs], plo[:, cs] = split(value)
 
 
 def final_kernel(
@@ -322,20 +348,12 @@
             flops=6 * products * m**3, bytes_accessed=12 * products * m * m, transcendentals=0
         )
 
-    wh = wl = coming = rows = None
+    rows = fresh = (amplitudes, control_index)
+    early = ()
     bit = 1
     while bit < order:
-        swap = [(i, i ^ bit) for i in range(order)]
-        fresh = rows if bit == 2 else coming
-        if bit > 1:
-            coming = lax.ppermute(rows, "fine", swap)
-            rows_next = (rows, coming)
-        else:
-            both = lax.ppermute((amplitudes, control_index), "fine", swap)
-            rows_next = [
-                jnp.concatenate([amps, picks.astype(f32)], axis=1)
-                for amps, picks in ((amplitudes, control_index), both)
-            ]
+        coming = lax.ppermute(rows, "fine", [(i, i ^ bit) for i in range(order)])
+        if bit == 1:
             table = pl.pallas_call(
                 load_kernel,
                 out_shape=pltpu.VMEM((kinds + 1, m, m), f32),
@@ -346,51 +364,52 @@
                 cost_estimate=cost(2),
                 name="load",
             )(outside(controls), outside(drift_term))
-        if bit > 1 and short:
-            past = () if wh is None else (inside(wh), inside(wl))
-            wh, wl = pl.pallas_call(
-                functools.partial(build_kernel, bit - fresh.shape[0]),
-                out_shape=(pltpu.VMEM((order, m, m), bf16),) * 2,
-                in_specs=[SMEM, VMEM] + [VMEM] * len(past),
+        elif short:
+            width = fresh[0].shape[0]
+            early = pl.pallas_call(
+                functools.partial(build_kernel, bit - width),
+                out_shape=(pltpu.VMEM((order // 2, m, m), bf16),) * 2,
+                in_specs=[SMEM, SMEM] + [VMEM] * (1 + len(early)),
                 out_specs=(VMEM, VMEM),
-                scratch_shapes=Work.shapes(m) * 2,
-                input_output_aliases={2: 0, 3: 1} if past else {},
+                scratch_shapes=Work.shapes(m) * width,
+                input_output_aliases={3: 0, 4: 1} if early else {},
                 compiler_params=params(BUILD_MIB),
-                cost_estimate=cost(4 * fresh.shape[0]),
+                cost_estimate=cost(4 * width),
                 name="build",
-            )(fresh, inside(table), *past)
-        rows = jnp.concatenate(rows_next, axis=0)
+            )(*fresh, inside(table), *map(inside, early))
+        rows = tuple(jnp.concatenate(pair, axis=0) for pair in zip(rows, coming))
+        fresh = rows if bit == 1 else coming
         bit *= 2
 
     if short:
-        kernel, taken = chain_kernel, (coming, table, wh, wl)
-        outs, aliases = (square, half, half) + (pltpu.VMEM((order, m, m), bf16),) * 2, {3: 3, 4: 4}
-        scratch = [half, half] + [pltpu.VMEM((2, m, m), bf16)] * 2
+        kernel, taken = chain_kernel, (table, *early)
+        outs = (square,) + (half,) * 4
+        halves = [pltpu.VMEM((order // 2, m, m), bf16)] * 2
+        scratch = halves * 2 + [pltpu.VMEM((2, m, m), bf16)] * 4 + Work.shapes(m) * (order // 2)
     else:
-        kernel, taken = long_kernel, (rows, table)
-        outs, aliases = (square, half, half), {}
-        scratch = [pltpu.VMEM((2, m, m), bf16), pltpu.VMEM((2, m, m), bf16), half, half]
-    run, lh, ll = pl.pallas_call(
-        functools.partial(kernel, order),
+        kernel, taken, fresh = functools.partial(long_kernel, order), (table,), rows
+        outs = (square, half, half)
+        scratch = [pltpu.VMEM((2, m, m), bf16)] * 2 + [half] * 2 + Work.shapes(m) * 2
+    run, *products = pl.pallas_call(
+        kernel,
         out_shape=outs,
-        in_specs=[SMEM, SMEM] + [VMEM] * (len(taken) - 1),
+        in_specs=[SMEM] * 3 + [VMEM] * len(taken),
         out_specs=(VMEM,) * len(outs),
-        scratch_shapes=[*scratch, *Work.shapes(m) * 2],
-        input_output_aliases=aliases,
+        scratch_shapes=scratch,
         compiler_params=params(CHAIN_MIB),
         cost_estimate=cost(23),
         name="chain",
-    )(place, taken[0], *map(inside, taken[1:]))[:3]
+    )(place, *fresh, *map(inside, taken))
     got = lax.ppermute(run, "coarse", [(0, 1), (1, 0)])
     turned = pl.pallas_call(
-        turn_kernel,
-        out_shape=(half,) * 6,
-        in_specs=[VMEM] * 2,
-        out_specs=(VMEM,) * 6,
+        functools.partial(turn_kernel, order // 2),
+        out_shape=(half,) * 8,
+        in_specs=[SMEM] + [VMEM] * (2 + len(products)),
+        out_specs=(VMEM,) * 8,
         compiler_params=params(TURN_MIB),
-        cost_estimate=cost(1),
+        cost_estimate=cost(2),
         name="turn",
-    )(inside(run), target)
+    )(place, inside(run), target, *map(inside, products))
     return pl.pallas_call(
         functools.partial(final_kernel, count),
         out_shape=jax.ShapeDtypeStruct((1, count), f32),
@@ -399,12 +418,12 @@
         scratch_shapes=[half] * 6 + [full] + [half] * 4,
         compiler_params=params(FINAL_MIB),
         name="final",
-    )(place, control_index, got, *map(inside, (*turned[:4], lh, ll, *turned[4:], table)))
+    )(place, control_index, got, *map(inside, (*turned, table)))
 
 
 LOAD_MIB = 4
 BUILD_MIB = 14
-CHAIN_MIB = 20
+CHAIN_MIB = 36
 TURN_MIB = 6
 FINAL_MIB = 12
 

time: 50.6 us -> 50.6 us (level)
  other arithmetic: 0.93 us -> 0.12 us
  starting transfers between devices: 7.77 us -> 8.48 us
  Pallas kernels: 40 us -> 40.6 us
  waiting for transfers between devices: 1.13 us -> 0.53 us
    convert_element_type x2 -> x0, other arithmetic: 0.69 us -> none  [on_device(): picks.astype(f32)]
    ppermute x1, waiting for transfers between devices: 1.12 us -> 0.51 us  [on_device(): got = lax.ppermute(run, 'coarse', [(0, 1), (1, 0)])]
    pallas_call x4, Pallas kernels: 30.3 us -> 30.9 us  [the longest x1 17.4 us: on_device(): pl.pallas_call(kernel, out_shape=outs, in_specs=[SMEM] * 3 + [VMEM] * len...]
    ppermute x4 -> x6, starting transfers between devices: 5.9 us -> 6.35 us  [on_device(): coming = lax.ppermute(rows, 'fine', [(i, i ^ bit) for i in range(order)])]
  transfers between devices with their start and end apart: 5 -> 7, of which waited for: 1 -> 1; matrix products, arithmetic and copies ran while one was open for 2% -> 0% of each run, Pallas kernels for 34% -> 36%
where the time goes in v4:
time: 50.6 us; the launch traced here: 50 us
  Pallas kernels  40.6 us (80%)
  starting transfers between devices  8.48 us (17%)
  waiting for transfers between devices  0.53 us (1%)
    pallas_call x1, Pallas kernels, on_device(): pl.pallas_call(kernel, out_shape=outs, in_specs=[SMEM] * 3 + [VMEM] * len...  17.4 us
    pallas_call x2, Pallas kernels, on_device(): pl.pallas_call(functools.partial(build_kernel, bit - width), out_shape=(p...  11.7 us
    ppermute x6, starting transfers between devices, on_device(): coming = lax.ppermute(rows, 'fine', [(i, i ^ bit) for i in range(order)])  6.35 us
    pallas_call x1, Pallas kernels, on_device(): pl.pallas_call(functools.partial(final_kernel, count), out_shape=jax.Shap...  5.32 us
    pallas_call x1, Pallas kernels, on_device(): pl.pallas_call(load_kernel, out_shape=pltpu.VMEM((kinds + 1, m, m), f32),...  4.37 us
    ppermute x1, starting transfers between devices, on_device(): got = lax.ppermute(run, 'coarse', [(0, 1), (1, 0)])  2.14 us
    pallas_call x1, Pallas kernels, on_device(): pl.pallas_call(functools.partial(turn_kernel, order // 2), out_shape=(hal...  1.76 us
  transfers between devices with their start and end apart: 7, of which 1 were waited for; matrix products, arithmetic and copies ran while one was open for 0% of the time, Pallas kernels for 36%

profile of v4, /device:TPU:1, one launch (start us, length us, event | category | flops | bytes accessed | tf_op | source)
XLA Modules:
  0.0 50.0 jit_solution(16591342343598937449)
XLA Ops:
  0.0 2.1 %collective-permute-start.3 = (s32[1,4]{1,0:T(1,128)}, s32[1,4]{1,0:T(1,128)S(1)}, u32[]{:S(2)}, u32[]{:S(2)}) collective-permute-start(s32[1,4]{1,0:T(1,128)} %picks.1), channel_id=1, source_target_pairs={{0,1},{1,0},{2,3},{3,2},{4,5},{5,4},{6,7},{7,6},{8,9},{9,8},{10,11... | collective-permute-start | bytes 56 | tf_op jit(solution)/shard_map/ppermute | solution.py:355
  2.1 0.0 collective-permute-start
  2.1 4.4 %load.1.table = f32[9,512,512]{2,1,0:T(8,128)S(1)} custom-call(f32[8,512,512]{2,1,0:T(8,128)} %controls.1, f32[512,512]{1,0:T(8,128)} %drift.1), custom_call_target="tpu_custom_call" | custom-call | flops 1610612736 | bytes 6291456 | tf_op jit(solution)/shard_map/load/pallas_call | solution.py:357
  6.5 0.1 pad_add_fusion.2.place
  6.5 0.0 collective-permute-done
  6.5 0.0 copy-done.2
  6.6 1.6 %collective-permute-start.1 = (f32[2,4]{1,0:T(2,128)S(1)}, f32[2,4]{1,0:T(2,128)S(1)}, u32[]{:S(2)}, u32[]{:S(2)}) collective-permute-start(f32[2,4]{1,0:T(2,128)S(1)} %pad_maximum_fusion.1.amps), channel_id=1, source_target_pairs={{0,2},{1,3},{2,0},{3,1},{4,6},{5,7},{6,4},{7,5},{8,10},{9,11},{10,... | collective-permute-start | bytes 104 | tf_op jit(solution)/shard_map/ppermute | solution.py:355
  8.1 0.0 collective-permute-done.3
  8.1 0.1 collective-permute-start.4
  8.2 5.9 %build.2 = (bf16[4,512,512]{2,1,0:T(8,128)(2,1)S(1)}, bf16[4,512,512]{2,1,0:T(8,128)(2,1)S(1)}) custom-call(f32[2,4]{1,0:T(2,128)S(1)} %pad_maximum_fusion.1.amps, s32[2,4]{1,0:T(2,128)S(1)} %pad_add_fusion.1.picks, f32[9,512,512]{2,1,0:T(8,128)S(1)} %load.1.table), custom_call_target="tpu_custom_call" | custom-call | flops 6442450944 | bytes 25165824 | tf_op jit(solution)/shard_map/build/pallas_call | solution.py:369
  14.1 0.0 collective-permute-done.4.picks
  14.1 2.5 %collective-permute-start.5 = (s32[4,4]{1,0:T(4,128)S(1)}, s32[4,4]{1,0:T(4,128)S(1)}, u32[]{:S(2)}, u32[]{:S(2)}) collective-permute-start(s32[4,4]{1,0:T(4,128)S(1)} %pad_add_fusion), channel_id=1, source_target_pairs={{0,4},{1,5},{2,6},{3,7},{4,0},{5,1},{6,2},{7,3},{8,12},{9,13},{10,... | collective-permute-start | bytes 200 | tf_op jit(solution)/shard_map/ppermute | solution.py:355
  16.6 0.0 collective-permute-done.1.amps
  16.7 0.1 collective-permute-start.2
  16.8 5.9 %build.3 = (bf16[4,512,512]{2,1,0:T(8,128)(2,1)S(1)}, bf16[4,512,512]{2,1,0:T(8,128)(2,1)S(1)}) custom-call(f32[2,4]{1,0:T(2,128)S(1)} %collective-permute-done.1.amps, s32[2,4]{1,0:T(2,128)S(1)} %collective-permute-done.4.picks, f32[9,512,512]{2,1,0:T(8,128)S(1)} %load.1.table, ...), custom_call_target="tpu_custom_call", output_to_operand_aliasing={{0}: (3, {}), {1}: (4, {})} | custom-call | flops 6442450944 | bytes 25165824 | tf_op jit(solution)/shard_map/build/pallas_call | solution.py:369
  22.6 0.0 collective-permute-done.5.picks
  22.6 0.0 collective-permute-done.2.amps
  22.6 0.0 copy-start.1
  22.7 17.4 %chain.1 = (f32[512,512]{1,0:T(8,128)S(1)}, bf16[512,512]{1,0:T(8,128)(2,1)S(1)}, bf16[512,512]{1,0:T(8,128)(2,1)S(1)}, bf16[512,512]{1,0:T(8,128)(2,1)S(1)}, bf16[512,512]{1,0:T(8,128)(2,1)S(1)}) custom-call(s32[2]{0:T(128)S(1)} %pad_add_fusion.2.place, f32[4,4]{1,0:T(4,128)S(1)} %collective-permute-done.2.amps, s32[4,4]{1,0:T(4,128)S(1)} %collective-permute-done.5.picks, ...), custom_call_target="tpu_custom_call" | custom-call | flops 18522046464 | bytes 72351744 | tf_op jit(solution)/shard_map/chain/pallas_call | solution.py:393
  40.1 2.1 %collective-permute-start.6 = (f32[512,512]{1,0:T(8,128)S(1)}, f32[512,512]{1,0:T(8,128)S(1)}, u32[]{:S(2)}, u32[]{:S(2)}) collective-permute-start(f32[512,512]{1,0:T(8,128)S(1)} %get-tuple-element.26.run), channel_id=1, source_target_pairs={{0,8},{8,0},{1,9},{9,1},{2,10},{10,2},{3,11},{11,3},{4,12},{12,4},... | collective-permute-start | bytes 3145736 | tf_op jit(solution)/shard_map/ppermute | solution.py:403
  42.2 0.0 copy-done.1
  42.2 1.8 %turn.1 = (bf16[512,512]{1,0:T(8,128)(2,1)S(1)}, bf16[512,512]{1,0:T(8,128)(2,1)S(1)}, bf16[512,512]{1,0:T(8,128)(2,1)S(1)}, bf16[512,512]{1,0:T(8,128)(2,1)S(1)...) custom-call(s32[2]{0:T(128)S(1)} %pad_add_fusion.2.place, ...), custom_call_target="tpu_custom_call" | custom-call | flops 1610612736 | bytes 6291456 | tf_op jit(solution)/shard_map/turn/pallas_call | solution.py:404
  44.0 0.5 %collective-permute-done.6.got = f32[512,512]{1,0:T(8,128)S(1)} collective-permute-done((f32[512,512]{1,0:T(8,128)S(1)}, f32[512,512]{1,0:T(8,128)S(1)}, u32[]{:S(2)}, u32[]{:S(2)}) %collective-permute-start.6) | collective-permute-done | bytes 1048608 | tf_op jit(solution)/shard_map/ppermute | solution.py:403
  44.5 5.3 %final.1 = f32[1,4]{1,0:T(1,128)} custom-call(s32[2]{0:T(128)S(1)} %pad_add_fusion.2.place, s32[1,4]{1,0:T(1,128)S(1)} %copy-done, f32[512,512]{1,0:T(8,128)S(1)} %collective-permute-done.6.got, bf16[512,512]{1,0:T(8,128)(2,1)S(1)} %get-tuple-element.31.turned_h, bf16[512,512]{1,0:T(8,128)(2,1)S(1)} %get-tuple-element.32.turned_l, ...), custom_call_target="tpu_custom_call" | custom-call | tf_op jit(solution)/shard_map/final/pallas_call | solution.py:413
  (7 shorter events, 0.0 us)
Async XLA Ops:
  0.0 8.1 %collective-permute-start.3 = (s32[1,4]{1,0:T(1,128)}, s32[1,4]{1,0:T(1,128)S(1)}, u32[]{:S(2)}, u32[]{:S(2)}) collective-permute-start(s32[1,4]{1,0:T(1,128)} %picks.1), channel_id=1, source_target_pairs={{0,1},{1,0},{2,3},{3,2},{4,5},{5,4},{6,7},{7,6},{8,9},{9,8},{10,11... | collective-permute-start | bytes 56 | tf_op jit(solution)/shard_map/ppermute | solution.py:355
  2.1 4.5 %collective-permute-start = (f32[1,4]{1,0:T(1,128)}, f32[1,4]{1,0:T(1,128)S(1)}, u32[]{:S(2)}, u32[]{:S(2)}) collective-permute-start(f32[1,4]{1,0:T(1,128)} %param.5), channel_id=1, source_target_pairs={{0,1},{1,0},{2,3},{3,2},{4,5},{5,4},{6,7},{7,6},{8,9},{9,8},{10,11... | collective-permute-start | bytes 56 | tf_op jit(solution)/shard_map/ppermute | solution.py:355
  2.1 4.5 %copy-start.2 = (f32[1,4]{1,0:T(1,128)S(1)}, f32[1,4]{1,0:T(1,128)}, u32[]{:S(2)}) copy-start(f32[1,4]{1,0:T(1,128)} %param.5) | copy-start | bytes 52
  2.1 6.1 %copy-start = (s32[1,4]{1,0:T(1,128)S(1)}, s32[1,4]{1,0:T(1,128)}, u32[]{:S(2)}) copy-start(s32[1,4]{1,0:T(1,128)} %picks.1) | copy-start | bytes 52
  6.6 10.1 %collective-permute-start.1 = (f32[2,4]{1,0:T(2,128)S(1)}, f32[2,4]{1,0:T(2,128)S(1)}, u32[]{:S(2)}, u32[]{:S(2)}) collective-permute-start(f32[2,4]{1,0:T(2,128)S(1)} %pad_maximum_fusion.1.amps), channel_id=1, source_target_pairs={{0,2},{1,3},{2,0},{3,1},{4,6},{5,7},{6,4},{7,5},{8,10},{9,11},{10,... | collective-permute-start | bytes 104 | tf_op jit(solution)/shard_map/ppermute | solution.py:355
  8.1 6.0 %collective-permute-start.4 = (s32[2,4]{1,0:T(2,128)S(1)}, s32[2,4]{1,0:T(2,128)S(1)}, u32[]{:S(2)}, u32[]{:S(2)}) collective-permute-start(s32[2,4]{1,0:T(2,128)S(1)} %pad_add_fusion.1.picks), channel_id=1, source_target_pairs={{0,2},{1,3},{2,0},{3,1},{4,6},{5,7},{6,4},{7,5},{8,10},{9,11},{10,... | collective-permute-start | bytes 104 | tf_op jit(solution)/shard_map/ppermute | solution.py:355
  14.1 8.5 %collective-permute-start.5 = (s32[4,4]{1,0:T(4,128)S(1)}, s32[4,4]{1,0:T(4,128)S(1)}, u32[]{:S(2)}, u32[]{:S(2)}) collective-permute-start(s32[4,4]{1,0:T(4,128)S(1)} %pad_add_fusion), channel_id=1, source_target_pairs={{0,4},{1,5},{2,6},{3,7},{4,0},{5,1},{6,2},{7,3},{8,12},{9,13},{10,... | collective-permute-start | bytes 200 | tf_op jit(solution)/shard_map/ppermute | solution.py:355
  16.7 6.0 %collective-permute-start.2 = (f32[4,4]{1,0:T(4,128)S(1)}, f32[4,4]{1,0:T(4,128)S(1)}, u32[]{:S(2)}, u32[]{:S(2)}) collective-permute-start(f32[4,4]{1,0:T(4,128)S(1)} %pad_maximum_fusion), channel_id=1, source_target_pairs={{0,4},{1,5},{2,6},{3,7},{4,0},{5,1},{6,2},{7,3},{8,12},{9,13},{10,... | collective-permute-start | bytes 200 | tf_op jit(solution)/shard_map/ppermute | solution.py:355
  22.6 19.6 %copy-start.1 = (f32[512,512]{1,0:T(8,128)S(1)}, f32[512,512]{1,0:T(8,128)}, u32[]{:S(2)}) copy-start(f32[512,512]{1,0:T(8,128)} %target.1) | copy-start | bytes 3145732
  40.1 4.4 %collective-permute-start.6 = (f32[512,512]{1,0:T(8,128)S(1)}, f32[512,512]{1,0:T(8,128)S(1)}, u32[]{:S(2)}, u32[]{:S(2)}) collective-permute-start(f32[512,512]{1,0:T(8,128)S(1)} %get-tuple-element.26.run), channel_id=1, source_target_pairs={{0,8},{8,0},{1,9},{9,1},{2,10},{10,2},{3,11},{11,3},{4,12},{12,4},... | collective-permute-start | bytes 3145736 | tf_op jit(solution)/shard_map/ppermute | solution.py:403

commit v5 on v4

--- a/solution.py
+++ b/solution.py
@@ -152,15 +152,15 @@
         return pltpu.make_async_copy(controls.at[k], table.at[k], sems.at[k])
 
     last = pltpu.make_async_copy(drift, table.at[kinds], sems.at[kinds])
-    for k in range(kinds):
-        copy(k).start()
-    last.start()
-
-    waits = [copy(k) for k in range(kinds)] + [last]
-    for at in range(0, kinds + 1, 3):
-        group = range(at, min(at + 3, kinds + 1))
+    copies = [copy(k) for k in range(kinds)] + [last]
+    groups = [range(at, min(at + 3, kinds + 1)) for at in range(0, kinds + 1, 3)]
+    for k in range(min(6, kinds + 1)):
+        copies[k].start()
+    for n, group in enumerate(groups):
         for k in group:
-            waits[k].wait()
+            copies[k].wait()
+        for k in groups[n + 2] if n + 2 < len(groups) else ():
+            copies[k].start()
         for k in group:
             skewed(table.at[k])
 
@@ -249,84 +249,108 @@
     lax.fori_loop(0, order // 2, pair, 0)
 
 
+def multiply_nt(ah, al, bh, bl, rows=slice(None)):
+    for cs in pieces(bh.shape[0], 256):
+        yield cs, (
+            dot_nt(ah[rows, :], bh[cs, :]) + dot_nt(ah[rows, :], bl[cs, :]) + dot_nt(al[rows, :], bh[cs, :])
+        )
+
+
 def turn_kernel(half, place, run, target, lh, ll, *refs):
-    below = refs[: len(refs) - 8]
-    vh, vl, bh, bl, ph, plo, th, tl = refs[len(refs) - 8 :]
+    below = refs[: len(refs) - 10]
+    eh, el, fh, fl, bh, bl, th, tl, ph, plo = refs[len(refs) - 10 :]
     m = run.shape[0]
-    for ti in pieces(m, 128):
-        bh[ti, :], bl[ti, :] = split(run[ti, :])
-        for tj in pieces(m, 128):
-            th[ti, tj], tl[ti, tj] = split(target[tj, ti].T)
-    for cs, value in multiply(th, tl, bh, bl):
-        vh[:, cs], vl[:, cs] = split(value)
-    first = True if not below else place[1] < half
-
-    @pl.when(first)
+    for rs in pieces(m, 32):
+        bh[rs, :], bl[rs, :] = split(run[rs, :])
+    later = place[1] >= half if below else False
+
+    @pl.when(jnp.logical_not(later))
     def _():
         for rs in pieces(m, 64):
             ph[rs, :], plo[rs, :] = lh[rs, :], ll[rs, :]
 
     if below:
 
-        @pl.when(place[1] >= half)
+        @pl.when(later)
         def _():
             for cs, value in multiply(lh, ll, *below):
                 ph[:, cs], plo[:, cs] = split(value)
 
-
-def final_kernel(
-    count, place, picks, got, turned_h, turned_l, run_h, run_l, local_h, local_l, th, tl, table, out,
-    gh, gl, ph, plo, vh, vl, x32, kh, kl, uh, ul,
-):
+    @pl.when(place[0] == 0)
+    def _():
+        for rs in pieces(m, 32):
+            th[rs, :], tl[rs, :] = split(target[rs, :])
+        for cs, value in multiply_nt(ph, plo, bh, bl):
+            eh[:, cs], el[:, cs] = split(value)
+        for cs, value in multiply_nt(ph, plo, th, tl):
+            fh[:, cs], fl[:, cs] = split(value)
+
+    @pl.when(place[0] != 0)
+    def _():
+        for ti in pieces(m, 128):
+            for tj in pieces(m, 128):
+                th[ti, tj], tl[ti, tj] = split(target[tj, ti].T)
+        for cs, value in multiply(th, tl, bh, bl):
+            eh[:, cs], el[:, cs] = split(value)
+        for rs in pieces(m, 64):
+            fh[rs, :], fl[rs, :] = ph[rs, :], plo[rs, :]
+
+
+def final_kernel(place, picks, got, eh, el, fh, fl, table, out, gh, gl, x32, ph, plo, kh, kl, uh, ul):
     m = got.shape[0]
-    coarse = place[0]
+    count = picks.shape[1]
+
+    def put(tiles_of):
+        totals = [jnp.zeros((8, min(m, 128)), f32)] * count
+        for ti, tj, tile in tiles_of:
+            for c in range(count):
+                part = table[picks[0, c], ti, tj] * tile
+                for at in range(0, part.shape[0], 8):
+                    totals[c] = totals[c] + part[at : at + 8, :]
+        for c in range(count):
+            out[0, c] = jnp.sum(totals[c])
+
     for rs in pieces(m, 32):
         gh[rs, :], gl[rs, :] = split(got[rs, :])
 
-    @pl.when(coarse == 0)
+    @pl.when(place[0] == 0)
     def _():
-        for rs in pieces(m, 64):
-            ph[rs, :], plo[rs, :] = local_h[rs, :], local_l[rs, :]
-        for cs in pieces(m, 256):
-            vh[:, cs], vl[:, cs] = split(dot3(th, tl, gh, gl, cs))
-        for cs in pieces(m, 256):
-            x32[:, cs] = dot3(vh, vl, run_h, run_l, cs)
-
-    @pl.when(coarse != 0)
+        for cs, value in multiply(fh, fl, gh, gl):
+            kh[:, cs], kl[:, cs] = split(value)
+        for cs, value in multiply_nt(eh, el, kh, kl):
+            x32[:, cs] = value
+
+        def tiles_of():
+            for ti, tj in lower_tiles(m):
+                yield ti, tj, x32[ti, tj] if ti == tj else x32[ti, tj] - x32[tj, ti].T
+
+        put(tiles_of())
+
+    @pl.when(place[0] != 0)
     def _():
-        for cs in pieces(m, 256):
-            x32[:, cs] = dot3(turned_h, turned_l, gh, gl, cs)
-        for cs in pieces(m, 256):
-            ph[:, cs], plo[:, cs] = split(dot3(local_h, local_l, gh, gl, cs))
-
-    for i, ti in enumerate(pieces(m, 128)):
-        for tj in pieces(m, 128)[: i + 1]:
+        for cs, value in multiply(eh, el, gh, gl):
+            x32[:, cs] = value
+        for cs, value in multiply(fh, fl, gh, gl):
+            ph[:, cs], plo[:, cs] = split(value)
+        for ti, tj in lower_tiles(m):
             value = 0.5 * (x32[tj, ti].T - x32[ti, tj])
             kh[ti, tj], kl[ti, tj] = split(value)
             if ti != tj:
                 kh[tj, ti], kl[tj, ti] = split(-value.T)
-    for cs in pieces(m, 256):
-        uh[:, cs], ul[:, cs] = split(dot3(ph, plo, kh, kl, cs))
-    totals = [jnp.zeros((8, 128), f32)] * count
-    for cs in pieces(m, 256):
-        for rs in pieces(m, 256):
-            if rs.start < cs.start:
-                continue
-            value = (
-                dot_nt(uh[rs, :], ph[cs, :]) + dot_nt(uh[rs, :], plo[cs, :]) + dot_nt(ul[rs, :], ph[cs, :])
-            )
-            for ti, tj in lower_tiles(m):
-                if not (rs.start <= ti.start < rs.stop and cs.start <= tj.start < cs.stop):
-                    continue
-                tile = value[ti.start - rs.start : ti.stop - rs.start, tj.start - cs.start : tj.stop - cs.start]
-                if ti != tj:
-                    tile = tile + tile
-                for c in range(count):
-                    part = table[picks[0, c], ti, tj] * tile
-                    for at in range(0, part.shape[0], 8):
-                        totals[c] = totals[c] + part[at : at + 8, :]
-    for c in range(count):
-        out[0, c] = jnp.sum(totals[c])
+        for cs, value in multiply(ph, plo, kh, kl):
+            uh[:, cs], ul[:, cs] = split(value)
+
+        def tiles_of():
+            for rs in pieces(m, 256):
+                for cs, value in multiply_nt(uh, ul, ph.at[: rs.stop], plo.at[: rs.stop], rs):
+                    for ti, tj in lower_tiles(m):
+                        if rs.start <= ti.start < rs.stop and cs.start <= tj.start < cs.stop:
+                            tile = value[
+                                ti.start - rs.start : ti.stop - rs.start, tj.start - cs.start : tj.stop - cs.start
+                            ]
+                            yield ti, tj, tile if ti == tj else tile + tile
+
+        put(tiles_of())
 
 
 def on_device(amplitudes, control_index, controls, drift_term, target):
@@ -403,19 +427,20 @@
     got = lax.ppermute(run, "coarse", [(0, 1), (1, 0)])
     turned = pl.pallas_call(
         functools.partial(turn_kernel, order // 2),
-        out_shape=(half,) * 8,
+        out_shape=(half,) * 4,
         in_specs=[SMEM] + [VMEM] * (2 + len(products)),
-        out_specs=(VMEM,) * 8,
+        out_specs=(VMEM,) * 4,
+        scratch_shapes=[half] * 6,
         compiler_params=params(TURN_MIB),
         cost_estimate=cost(2),
         name="turn",
     )(place, inside(run), target, *map(inside, products))
     return pl.pallas_call(
-        functools.partial(final_kernel, count),
+        final_kernel,
         out_shape=jax.ShapeDtypeStruct((1, count), f32),
-        in_specs=[SMEM, SMEM] + [VMEM] * 10,
+        in_specs=[SMEM, SMEM] + [VMEM] * 6,
         out_specs=SMEM,
-        scratch_shapes=[half] * 6 + [full] + [half] * 4,
+        scratch_shapes=[half] * 2 + [full] + [half] * 6,
         compiler_params=params(FINAL_MIB),
         name="final",
     )(place, control_index, got, *map(inside, (*turned, table)))

time: 50.6 us -> 50.2 us (level)
  transfers between devices with their start and end apart: 7 -> 7, of which waited for: 1 -> 1; matrix products, arithmetic and copies ran while one was open for 0% -> 0% of each run, Pallas kernels for 36% -> 37%
where the time goes in v5:
time: 50.2 us; the launch traced here: 49.9 us
  Pallas kernels  40.7 us (81%)
  starting transfers between devices  8.49 us (17%)
    pallas_call x1, Pallas kernels, on_device(): pl.pallas_call(kernel, out_shape=outs, in_specs=[SMEM] * 3 + [VMEM] * len...  17.4 us
    pallas_call x2, Pallas kernels, on_device(): pl.pallas_call(functools.partial(build_kernel, bit - width), out_shape=(p...  11.7 us
    ppermute x6, starting transfers between devices, on_device(): coming = lax.ppermute(rows, 'fine', [(i, i ^ bit) for i in range(order)])  6.35 us
    pallas_call x1, Pallas kernels, on_device(): pl.pallas_call(final_kernel, out_shape=jax.ShapeDtypeStruct((1, count), f...  5 us
    pallas_call x1, Pallas kernels, on_device(): pl.pallas_call(load_kernel, out_shape=pltpu.VMEM((kinds + 1, m, m), f32),...  4.63 us
    ppermute x1, starting transfers between devices, on_device(): got = lax.ppermute(run, 'coarse', [(0, 1), (1, 0)])  2.14 us
    pallas_call x1, Pallas kernels, on_device(): pl.pallas_call(functools.partial(turn_kernel, order // 2), out_shape=(hal...  1.91 us
  transfers between devices with their start and end apart: 7, of which 1 were waited for; matrix products, arithmetic and copies ran while one was open for 0% of the time, Pallas kernels for 37%

profile of v5, /device:TPU:1, one launch (start us, length us, event | category | flops | bytes accessed | tf_op | source)
XLA Modules:
  0.0 49.9 jit_solution(8159152907313801254)
XLA Ops:
  0.0 2.1 %collective-permute-start.3 = (s32[1,4]{1,0:T(1,128)}, s32[1,4]{1,0:T(1,128)S(1)}, u32[]{:S(2)}, u32[]{:S(2)}) collective-permute-start(s32[1,4]{1,0:T(1,128)} %picks.1), channel_id=1, source_target_pairs={{0,1},{1,0},{2,3},{3,2},{4,5},{5,4},{6,7},{7,6},{8,9},{9,8},{10,11... | collective-permute-start | bytes 56 | tf_op jit(solution)/shard_map/ppermute | solution.py:379
  2.1 0.0 collective-permute-start
  2.1 4.6 %load.1.table = f32[9,512,512]{2,1,0:T(8,128)S(1)} custom-call(f32[8,512,512]{2,1,0:T(8,128)} %controls.1, f32[512,512]{1,0:T(8,128)} %drift.1), custom_call_target="tpu_custom_call" | custom-call | flops 1610612736 | bytes 6291456 | tf_op jit(solution)/shard_map/load/pallas_call | solution.py:381
  6.7 0.1 pad_add_fusion.2.place
  6.8 0.0 collective-permute-done
  6.8 0.0 copy-done.2
  6.8 1.6 %collective-permute-start.1 = (f32[2,4]{1,0:T(2,128)S(1)}, f32[2,4]{1,0:T(2,128)S(1)}, u32[]{:S(2)}, u32[]{:S(2)}) collective-permute-start(f32[2,4]{1,0:T(2,128)S(1)} %pad_maximum_fusion.1.amps), channel_id=1, source_target_pairs={{0,2},{1,3},{2,0},{3,1},{4,6},{5,7},{6,4},{7,5},{8,10},{9,11},{10,... | collective-permute-start | bytes 104 | tf_op jit(solution)/shard_map/ppermute | solution.py:379
  8.4 0.0 collective-permute-done.3
  8.4 0.0 copy-done
  8.4 0.1 collective-permute-start.4
  8.5 5.9 %build.2 = (bf16[4,512,512]{2,1,0:T(8,128)(2,1)S(1)}, bf16[4,512,512]{2,1,0:T(8,128)(2,1)S(1)}) custom-call(f32[2,4]{1,0:T(2,128)S(1)} %pad_maximum_fusion.1.amps, s32[2,4]{1,0:T(2,128)S(1)} %pad_add_fusion.1.picks, f32[9,512,512]{2,1,0:T(8,128)S(1)} %load.1.table), custom_call_target="tpu_custom_call" | custom-call | flops 6442450944 | bytes 25165824 | tf_op jit(solution)/shard_map/build/pallas_call | solution.py:393
  14.4 0.0 collective-permute-done.4.picks
  14.4 2.5 %collective-permute-start.5 = (s32[4,4]{1,0:T(4,128)S(1)}, s32[4,4]{1,0:T(4,128)S(1)}, u32[]{:S(2)}, u32[]{:S(2)}) collective-permute-start(s32[4,4]{1,0:T(4,128)S(1)} %pad_add_fusion), channel_id=1, source_target_pairs={{0,4},{1,5},{2,6},{3,7},{4,0},{5,1},{6,2},{7,3},{8,12},{9,13},{10,... | collective-permute-start | bytes 200 | tf_op jit(solution)/shard_map/ppermute | solution.py:379
  16.9 0.0 collective-permute-done.1.amps
  16.9 0.1 collective-permute-start.2
  17.0 5.9 %build.3 = (bf16[4,512,512]{2,1,0:T(8,128)(2,1)S(1)}, bf16[4,512,512]{2,1,0:T(8,128)(2,1)S(1)}) custom-call(f32[2,4]{1,0:T(2,128)S(1)} %collective-permute-done.1.amps, s32[2,4]{1,0:T(2,128)S(1)} %collective-permute-done.4.picks, f32[9,512,512]{2,1,0:T(8,128)S(1)} %load.1.table, ...), custom_call_target="tpu_custom_call", output_to_operand_aliasing={{0}: (3, {}), {1}: (4, {})} | custom-call | flops 6442450944 | bytes 25165824 | tf_op jit(solution)/shard_map/build/pallas_call | solution.py:393
  22.9 0.0 collective-permute-done.5.picks
  22.9 0.0 collective-permute-done.2.amps
  22.9 0.0 copy-start.1
  22.9 17.4 %chain.1 = (f32[512,512]{1,0:T(8,128)S(1)}, bf16[512,512]{1,0:T(8,128)(2,1)S(1)}, bf16[512,512]{1,0:T(8,128)(2,1)S(1)}, bf16[512,512]{1,0:T(8,128)(2,1)S(1)}, bf16[512,512]{1,0:T(8,128)(2,1)S(1)}) custom-call(s32[2]{0:T(128)S(1)} %pad_add_fusion.2.place, f32[4,4]{1,0:T(4,128)S(1)} %collective-permute-done.2.amps, s32[4,4]{1,0:T(4,128)S(1)} %collective-permute-done.5.picks, ...), custom_call_target="tpu_custom_call" | custom-call | flops 18522046464 | bytes 72351744 | tf_op jit(solution)/shard_map/chain/pallas_call | solution.py:417
  40.3 2.1 %collective-permute-start.6 = (f32[512,512]{1,0:T(8,128)S(1)}, f32[512,512]{1,0:T(8,128)S(1)}, u32[]{:S(2)}, u32[]{:S(2)}) collective-permute-start(f32[512,512]{1,0:T(8,128)S(1)} %get-tuple-element.22.run), channel_id=1, source_target_pairs={{0,8},{8,0},{1,9},{9,1},{2,10},{10,2},{3,11},{11,3},{4,12},{12,4},... | collective-permute-start | bytes 3145736 | tf_op jit(solution)/shard_map/ppermute | solution.py:427
  42.5 1.9 %turn.1 = (bf16[512,512]{1,0:T(8,128)(2,1)S(1)}, bf16[512,512]{1,0:T(8,128)(2,1)S(1)}, bf16[512,512]{1,0:T(8,128)(2,1)S(1)}, bf16[512,512]{1,0:T(8,128)(2,1)S(1)}) custom-call(s32[2]{0:T(128)S(1)} %pad_add_fusion.2.place, f32[512,512]{1,0:T(8,128)S(1)} %get-tuple-element.22.run, f32[512,512]{1,0:T(8,128)S(1)} %copy-done.1, ...), custom_call_target="tpu_custom_call" | custom-call | flops 1610612736 | bytes 6291456 | tf_op jit(solution)/shard_map/turn/pallas_call | solution.py:428
  44.4 0.4 collective-permute-done.6.got
  44.7 5.0 %final.1 = f32[1,4]{1,0:T(1,128)} custom-call(s32[2]{0:T(128)S(1)} %pad_add_fusion.2.place, s32[1,4]{1,0:T(1,128)S(1)} %copy-done, f32[512,512]{1,0:T(8,128)S(1)} %collective-permute-done.6.got, bf16[512,512]{1,0:T(8,128)(2,1)S(1)} %get-tuple-element.27.eh, bf16[512,512]{1,0:T(8,128)(2,1)S(1)} %get-tuple-element.28.el, ...), custom_call_target="tpu_custom_call" | custom-call | tf_op jit(solution)/shard_map/final/pallas_call | solution.py:438
  (7 shorter events, 0.0 us)
Async XLA Ops:
  0.0 8.4 %collective-permute-start.3 = (s32[1,4]{1,0:T(1,128)}, s32[1,4]{1,0:T(1,128)S(1)}, u32[]{:S(2)}, u32[]{:S(2)}) collective-permute-start(s32[1,4]{1,0:T(1,128)} %picks.1), channel_id=1, source_target_pairs={{0,1},{1,0},{2,3},{3,2},{4,5},{5,4},{6,7},{7,6},{8,9},{9,8},{10,11... | collective-permute-start | bytes 56 | tf_op jit(solution)/shard_map/ppermute | solution.py:379
  2.1 4.7 %collective-permute-start = (f32[1,4]{1,0:T(1,128)}, f32[1,4]{1,0:T(1,128)S(1)}, u32[]{:S(2)}, u32[]{:S(2)}) collective-permute-start(f32[1,4]{1,0:T(1,128)} %param.5), channel_id=1, source_target_pairs={{0,1},{1,0},{2,3},{3,2},{4,5},{5,4},{6,7},{7,6},{8,9},{9,8},{10,11... | collective-permute-start | bytes 56 | tf_op jit(solution)/shard_map/ppermute | solution.py:379
  2.1 4.7 %copy-start.2 = (f32[1,4]{1,0:T(1,128)S(1)}, f32[1,4]{1,0:T(1,128)}, u32[]{:S(2)}) copy-start(f32[1,4]{1,0:T(1,128)} %param.5) | copy-start | bytes 52
  2.1 6.3 %copy-start = (s32[1,4]{1,0:T(1,128)S(1)}, s32[1,4]{1,0:T(1,128)}, u32[]{:S(2)}) copy-start(s32[1,4]{1,0:T(1,128)} %picks.1) | copy-start | bytes 52
  6.8 10.1 %collective-permute-start.1 = (f32[2,4]{1,0:T(2,128)S(1)}, f32[2,4]{1,0:T(2,128)S(1)}, u32[]{:S(2)}, u32[]{:S(2)}) collective-permute-start(f32[2,4]{1,0:T(2,128)S(1)} %pad_maximum_fusion.1.amps), channel_id=1, source_target_pairs={{0,2},{1,3},{2,0},{3,1},{4,6},{5,7},{6,4},{7,5},{8,10},{9,11},{10,... | collective-permute-start | bytes 104 | tf_op jit(solution)/shard_map/ppermute | solution.py:379
  8.4 6.0 %collective-permute-start.4 = (s32[2,4]{1,0:T(2,128)S(1)}, s32[2,4]{1,0:T(2,128)S(1)}, u32[]{:S(2)}, u32[]{:S(2)}) collective-permute-start(s32[2,4]{1,0:T(2,128)S(1)} %pad_add_fusion.1.picks), channel_id=1, source_target_pairs={{0,2},{1,3},{2,0},{3,1},{4,6},{5,7},{6,4},{7,5},{8,10},{9,11},{10,... | collective-permute-start | bytes 104 | tf_op jit(solution)/shard_map/ppermute | solution.py:379
  14.4 8.5 %collective-permute-start.5 = (s32[4,4]{1,0:T(4,128)S(1)}, s32[4,4]{1,0:T(4,128)S(1)}, u32[]{:S(2)}, u32[]{:S(2)}) collective-permute-start(s32[4,4]{1,0:T(4,128)S(1)} %pad_add_fusion), channel_id=1, source_target_pairs={{0,4},{1,5},{2,6},{3,7},{4,0},{5,1},{6,2},{7,3},{8,12},{9,13},{10,... | collective-permute-start | bytes 200 | tf_op jit(solution)/shard_map/ppermute | solution.py:379
  16.9 6.0 %collective-permute-start.2 = (f32[4,4]{1,0:T(4,128)S(1)}, f32[4,4]{1,0:T(4,128)S(1)}, u32[]{:S(2)}, u32[]{:S(2)}) collective-permute-start(f32[4,4]{1,0:T(4,128)S(1)} %pad_maximum_fusion), channel_id=1, source_target_pairs={{0,4},{1,5},{2,6},{3,7},{4,0},{5,1},{6,2},{7,3},{8,12},{9,13},{10,... | collective-permute-start | bytes 200 | tf_op jit(solution)/shard_map/ppermute | solution.py:379
  22.9 19.6 %copy-start.1 = (f32[512,512]{1,0:T(8,128)S(1)}, f32[512,512]{1,0:T(8,128)}, u32[]{:S(2)}) copy-start(f32[512,512]{1,0:T(8,128)} %target.1) | copy-start | bytes 3145732
  40.3 4.4 %collective-permute-start.6 = (f32[512,512]{1,0:T(8,128)S(1)}, f32[512,512]{1,0:T(8,128)S(1)}, u32[]{:S(2)}, u32[]{:S(2)}) collective-permute-start(f32[512,512]{1,0:T(8,128)S(1)} %get-tuple-element.22.run), channel_id=1, source_target_pairs={{0,8},{8,0},{1,9},{9,1},{2,10},{10,2},{3,11},{11,3},{4,12},{12,4},... | collective-permute-start | bytes 3145736 | tf_op jit(solution)/shard_map/ppermute | solution.py:427

commit v6 on v5

--- a/solution.py
+++ b/solution.py
@@ -133,10 +133,12 @@
         return [pltpu.VMEM((m, m), f32)] * 2 + [pltpu.VMEM((m, m), bf16)] * 8
 
 
-def propagators(amps, picks, picked, works, table, wh, wl, slots):
-    count = amps.shape[1]
+def propagators(rows, picked, works, table, wh, wl, slots):
+    count = rows.shape[1] // 2
     for row, s in zip(picked, works):
-        generator([amps[row, c] for c in range(count)], [picks[row, c] for c in range(count)], table, s)
+        amps = [rows[row, c] for c in range(count)]
+        picks = [rows[row, count + c].astype(jnp.int32) for c in range(count)]
+        generator(amps, picks, table, s)
     for s in works:
         square_step(s)
     for s in works:
@@ -153,14 +155,12 @@
 
     last = pltpu.make_async_copy(drift, table.at[kinds], sems.at[kinds])
     copies = [copy(k) for k in range(kinds)] + [last]
-    groups = [range(at, min(at + 3, kinds + 1)) for at in range(0, kinds + 1, 3)]
-    for k in range(min(6, kinds + 1)):
-        copies[k].start()
-    for n, group in enumerate(groups):
+    for each in copies:
+        each.start()
+    for at in range(0, kinds + 1, 3):
+        group = range(at, min(at + 3, kinds + 1))
         for k in group:
             copies[k].wait()
-        for k in groups[n + 2] if n + 2 < len(groups) else ():
-            copies[k].start()
         for k in group:
             skewed(table.at[k])
 
@@ -170,12 +170,12 @@
     return [Work(scratch[at : at + size]) for at in range(0, len(scratch), size)]
 
 
-def build_kernel(first, amps, picks, table, *refs):
+def build_kernel(first, rows, table, *refs):
     size = len(Work.names)
-    width = amps.shape[0]
+    width = rows.shape[0]
     wh, wl = refs[-2 - width * size : -width * size]
     slots = [first + n for n in range(width)]
-    propagators(amps, picks, range(width), works_of(refs[-width * size :]), table, wh, wl, slots)
+    propagators(rows, range(width), works_of(refs[-width * size :]), table, wh, wl, slots)
 
 
 def multiply(ah, al, bh, bl):
@@ -184,14 +184,14 @@
 
 
 def chain_kernel(
-    place, amps, picks, table, early_h, early_l, run, lh, ll, oh, ol,
+    place, rows, table, early_h, early_l, run, lh, ll, oh, ol,
     wh, wl, th, tl, qh, ql, bh, bl, *scratch
 ):
     half, m = early_h.shape[:2]
     fine = place[1]
     inner = fine & (half - 1)
     upper = jnp.where(fine < half, 1, 0)
-    propagators(amps, picks, range(half), works_of(scratch), table, wh, wl, range(half))
+    propagators(rows, range(half), works_of(scratch), table, wh, wl, range(half))
     for rs in pieces(m, 64):
         high, low = early_h[inner, rs, :], early_l[inner, rs, :]
         qh[0, rs, :], ql[0, rs, :] = high, low
@@ -221,8 +221,13 @@
     for rs in pieces(m, 64):
         oh[rs, :], ol[rs, :] = qh[1, rs, :], ql[1, rs, :]
 
-
-def long_kernel(order, place, amps, picks, table, run, lh, ll, wh, wl, rh, rl, *scratch):
+    @pl.when((place[0] != 0) & (fine >= half))
+    def _():
+        for cs, value in multiply(bh.at[0], bl.at[0], qh.at[1], ql.at[1]):
+            lh[:, cs], ll[:, cs] = split(value)
+
+
+def long_kernel(order, place, rows, table, run, lh, ll, wh, wl, rh, rl, *scratch):
     works = works_of(scratch)
     m = run.shape[0]
     fine = place[1]
@@ -233,7 +238,7 @@
 
     def pair(n, carry):
         steps = [2 * n, 2 * n + 1]
-        propagators(amps, picks, [step ^ fine for step in steps], works, table, wh, wl, range(2))
+        propagators(rows, [step ^ fine for step in steps], works, table, wh, wl, range(2))
         for k, step in enumerate(steps):
             for cs, value in multiply(wh.at[k], wl.at[k], rh, rl):
                 run[:, cs] = value
@@ -262,7 +267,7 @@
     m = run.shape[0]
     for rs in pieces(m, 32):
         bh[rs, :], bl[rs, :] = split(run[rs, :])
-    later = place[1] >= half if below else False
+    later = (place[0] == 0) & (place[1] >= half) if below else False
 
     @pl.when(jnp.logical_not(later))
     def _():
@@ -372,11 +377,15 @@
             flops=6 * products * m**3, bytes_accessed=12 * products * m * m, transcendentals=0
         )
 
-    rows = fresh = (amplitudes, control_index)
+    rows = fresh = coming = None
     early = ()
     bit = 1
     while bit < order:
-        coming = lax.ppermute(rows, "fine", [(i, i ^ bit) for i in range(order)])
+        swap = [(i, i ^ bit) for i in range(order)]
+        if bit == 1:
+            pairs = (amplitudes, control_index), lax.ppermute((amplitudes, control_index), "fine", swap)
+        else:
+            coming = lax.ppermute(rows, "fine", swap)
         if bit == 1:
             table = pl.pallas_call(
                 load_kernel,
@@ -389,20 +398,23 @@
                 name="load",
             )(outside(controls), outside(drift_term))
         elif short:
-            width = fresh[0].shape[0]
+            width = fresh.shape[0]
             early = pl.pallas_call(
                 functools.partial(build_kernel, bit - width),
                 out_shape=(pltpu.VMEM((order // 2, m, m), bf16),) * 2,
-                in_specs=[SMEM, SMEM] + [VMEM] * (1 + len(early)),
+                in_specs=[SMEM] + [VMEM] * (1 + len(early)),
                 out_specs=(VMEM, VMEM),
                 scratch_shapes=Work.shapes(m) * width,
-                input_output_aliases={3: 0, 4: 1} if early else {},
+                input_output_aliases={2: 0, 3: 1} if early else {},
                 compiler_params=params(BUILD_MIB),
                 cost_estimate=cost(4 * width),
                 name="build",
-            )(*fresh, inside(table), *map(inside, early))
-        rows = tuple(jnp.concatenate(pair, axis=0) for pair in zip(rows, coming))
-        fresh = rows if bit == 1 else coming
+            )(fresh, inside(table), *map(inside, early))
+        if bit == 1:
+            amps, picks = lax.optimization_barrier([jnp.concatenate(each, axis=0) for each in zip(*pairs)])
+            rows = fresh = jnp.concatenate([amps, picks.astype(f32)], axis=1)
+        else:
+            rows, fresh = jnp.concatenate([rows, coming], axis=0), coming
         bit *= 2
 
     if short:
@@ -417,13 +429,13 @@
     run, *products = pl.pallas_call(
         kernel,
         out_shape=outs,
-        in_specs=[SMEM] * 3 + [VMEM] * len(taken),
+        in_specs=[SMEM] * 2 + [VMEM] * len(taken),
         out_specs=(VMEM,) * len(outs),
         scratch_shapes=scratch,
         compiler_params=params(CHAIN_MIB),
         cost_estimate=cost(23),
         name="chain",
-    )(place, *fresh, *map(inside, taken))
+    )(place, fresh, *map(inside, taken))
     got = lax.ppermute(run, "coarse", [(0, 1), (1, 0)])
     turned = pl.pallas_call(
         functools.partial(turn_kernel, order // 2),

time: 50.2 us -> 48.7 us (0.970)
  Pallas kernels: 40.7 us -> 39.9 us
  starting transfers between devices: 8.49 us -> 7.76 us
    ppermute x6 -> x4, starting transfers between devices: 6.35 us -> 5.9 us  [the longest x2 3.82 us: on_device(): coming = lax.ppermute(rows, 'fine', swap)]
  transfers between devices with their start and end apart: 7 -> 5, of which waited for: 1 -> 1; matrix products, arithmetic and copies ran while one was open for 0% -> 0% of each run, Pallas kernels for 37% -> 37%
where the time goes in v6:
time: 48.7 us; the launch traced here: 48.6 us
  Pallas kernels  39.9 us (82%)
  starting transfers between devices  7.76 us (16%)
    pallas_call x1, Pallas kernels, on_device(): pl.pallas_call(kernel, out_shape=outs, in_specs=[SMEM] * 2 + [VMEM] * len...  17.1 us
    pallas_call x2, Pallas kernels, on_device(): pl.pallas_call(functools.partial(build_kernel, bit - width), out_shape=(p...  11.5 us
    pallas_call x1, Pallas kernels, on_device(): pl.pallas_call(final_kernel, out_shape=jax.ShapeDtypeStruct((1, count), f...  4.99 us
    pallas_call x1, Pallas kernels, on_device(): pl.pallas_call(load_kernel, out_shape=pltpu.VMEM((kinds + 1, m, m), f32),...  4.37 us
    ppermute x2, starting transfers between devices, on_device(): coming = lax.ppermute(rows, 'fine', swap)  3.82 us
    ppermute x2, starting transfers between devices, on_device(): lax.ppermute((amplitudes, control_index), 'fine', swap)  2.08 us
    pallas_call x1, Pallas kernels, on_device(): pl.pallas_call(functools.partial(turn_kernel, order // 2), out_shape=(hal...  1.91 us
    ppermute x1, starting transfers between devices, on_device(): got = lax.ppermute(run, 'coarse', [(0, 1), (1, 0)])  1.86 us
  transfers between devices with their start and end apart: 5, of which 1 were waited for; matrix products, arithmetic and copies ran while one was open for 0% of the time, Pallas kernels for 37%

profile of v6, /device:TPU:1, one launch (start us, length us, event | category | flops | bytes accessed | tf_op | source)
XLA Modules:
  0.0 48.6 jit_solution(13415018314667122377)
XLA Ops:
  0.0 2.1 %collective-permute-start.1 = (s32[1,4]{1,0:T(1,128)}, s32[1,4]{1,0:T(1,128)S(1)}, u32[]{:S(2)}, u32[]{:S(2)}) collective-permute-start(s32[1,4]{1,0:T(1,128)} %picks.1), channel_id=1, source_target_pairs={{0,1},{1,0},{2,3},{3,2},{4,5},{5,4},{6,7},{7,6},{8,9},{9,8},{10,11... | collective-permute-start | bytes 56 | tf_op jit(solution)/shard_map/ppermute | solution.py:386
  2.1 0.0 collective-permute-start
  2.1 0.0 copy-start
  2.1 4.4 %load.1.table = f32[9,512,512]{2,1,0:T(8,128)S(1)} custom-call(f32[8,512,512]{2,1,0:T(8,128)} %controls.1, f32[512,512]{1,0:T(8,128)} %drift.1), custom_call_target="tpu_custom_call" | custom-call | flops 1610612736 | bytes 6291456 | tf_op jit(solution)/shard_map/load/pallas_call | solution.py:390
  6.5 0.1 pad_add_fusion.1.place
  6.5 0.0 collective-permute-done.1
  6.5 0.0 copy-done
  6.6 0.0 collective-permute-done
  6.6 0.0 copy-done.2
  6.6 0.1 pad_maximum_fusion.2.rows
  6.7 1.5 %collective-permute-start.2 = (f32[2,8]{1,0:T(2,128)S(1)}, f32[2,8]{1,0:T(2,128)S(1)}, u32[]{:S(2)}, u32[]{:S(2)}) collective-permute-start(f32[2,8]{1,0:T(2,128)S(1)} %pad_maximum_fusion.2.rows), channel_id=1, source_target_pairs={{0,2},{1,3},{2,0},{3,1},{4,6},{5,7},{6,4},{7,5},{8,10},{9,11},{10,... | collective-permute-start | bytes 200 | tf_op jit(solution)/shard_map/ppermute | solution.py:388
  8.2 5.7 %build.2 = (bf16[4,512,512]{2,1,0:T(8,128)(2,1)S(1)}, bf16[4,512,512]{2,1,0:T(8,128)(2,1)S(1)}) custom-call(f32[2,8]{1,0:T(2,128)S(1)} %pad_maximum_fusion.2.rows, f32[9,512,512]{2,1,0:T(8,128)S(1)} %load.1.table), custom_call_target="tpu_custom_call" | custom-call | flops 6442450944 | bytes 25165824 | tf_op jit(solution)/shard_map/build/pallas_call | solution.py:402
  13.9 0.0 collective-permute-done.2.rows
  14.0 0.1 pad_maximum_fusion
  14.0 2.3 %collective-permute-start.3 = (f32[4,8]{1,0:T(4,128)S(1)}, f32[4,8]{1,0:T(4,128)S(1)}, u32[]{:S(2)}, u32[]{:S(2)}) collective-permute-start(f32[4,8]{1,0:T(4,128)S(1)} %pad_maximum_fusion), channel_id=1, source_target_pairs={{0,4},{1,5},{2,6},{3,7},{4,0},{5,1},{6,2},{7,3},{8,12},{9,13},{10,... | collective-permute-start | bytes 392 | tf_op jit(solution)/shard_map/ppermute | solution.py:388
  16.4 5.7 %build.3 = (bf16[4,512,512]{2,1,0:T(8,128)(2,1)S(1)}, bf16[4,512,512]{2,1,0:T(8,128)(2,1)S(1)}) custom-call(f32[2,8]{1,0:T(2,128)S(1)} %collective-permute-done.2.rows, f32[9,512,512]{2,1,0:T(8,128)S(1)} %load.1.table, bf16[4,512,512]{2,1,0:T(8,128)(2,1)S(1)} %get-tuple-element.22.refs_0_, ...), custom_call_target="tpu_custom_call", output_to_operand_aliasing={{0}: (2, {}), {1}: (3, {})} | custom-call | flops 6442450944 | bytes 25165824 | tf_op jit(solution)/shard_map/build/pallas_call | solution.py:402
  22.1 0.0 collective-permute-done.3.rows
  22.1 0.0 copy-start.1
  22.1 17.1 %chain.1 = (f32[512,512]{1,0:T(8,128)S(1)}, bf16[512,512]{1,0:T(8,128)(2,1)S(1)}, bf16[512,512]{1,0:T(8,128)(2,1)S(1)}, bf16[512,512]{1,0:T(8,128)(2,1)S(1)}, bf16[512,512]{1,0:T(8,128)(2,1)S(1)}) custom-call(s32[2]{0:T(128)S(1)} %pad_add_fusion.1.place, f32[4,8]{1,0:T(4,128)S(1)} %collective-permute-done.3.rows, f32[9,512,512]{2,1,0:T(8,128)S(1)} %load.1.table, ...), custom_call_target="tpu_custom_call" | custom-call | flops 18522046464 | bytes 72351744 | tf_op jit(solution)/shard_map/chain/pallas_call | solution.py:429
  39.2 1.9 %collective-permute-start.4 = (f32[512,512]{1,0:T(8,128)S(1)}, f32[512,512]{1,0:T(8,128)S(1)}, u32[]{:S(2)}, u32[]{:S(2)}) collective-permute-start(f32[512,512]{1,0:T(8,128)S(1)} %get-tuple-element.26.run), channel_id=1, source_target_pairs={{0,8},{8,0},{1,9},{9,1},{2,10},{10,2},{3,11},{11,3},{4,12},{12,4},... | collective-permute-start | bytes 3145736 | tf_op jit(solution)/shard_map/ppermute | solution.py:439
  41.1 0.0 copy-done.1
  41.1 1.9 %turn.1 = (bf16[512,512]{1,0:T(8,128)(2,1)S(1)}, bf16[512,512]{1,0:T(8,128)(2,1)S(1)}, bf16[512,512]{1,0:T(8,128)(2,1)S(1)}, bf16[512,512]{1,0:T(8,128)(2,1)S(1)}) custom-call(s32[2]{0:T(128)S(1)} %pad_add_fusion.1.place, f32[512,512]{1,0:T(8,128)S(1)} %get-tuple-element.26.run, f32[512,512]{1,0:T(8,128)S(1)} %copy-done.1, ...), custom_call_target="tpu_custom_call" | custom-call | flops 1610612736 | bytes 6291456 | tf_op jit(solution)/shard_map/turn/pallas_call | solution.py:440
  43.0 0.4 collective-permute-done.4.got
  43.4 5.0 %final.1 = f32[1,4]{1,0:T(1,128)} custom-call(s32[2]{0:T(128)S(1)} %pad_add_fusion.1.place, s32[1,4]{1,0:T(1,128)S(1)} %copy-done, f32[512,512]{1,0:T(8,128)S(1)} %collective-permute-done.4.got, bf16[512,512]{1,0:T(8,128)(2,1)S(1)} %get-tuple-element.31.eh, bf16[512,512]{1,0:T(8,128)(2,1)S(1)} %get-tuple-element.32.el, ...), custom_call_target="tpu_custom_call" | custom-call | tf_op jit(solution)/shard_map/final/pallas_call | solution.py:450
  (4 shorter events, 0.0 us)
Async XLA Ops:
  0.0 6.5 %collective-permute-start.1 = (s32[1,4]{1,0:T(1,128)}, s32[1,4]{1,0:T(1,128)S(1)}, u32[]{:S(2)}, u32[]{:S(2)}) collective-permute-start(s32[1,4]{1,0:T(1,128)} %picks.1), channel_id=1, source_target_pairs={{0,1},{1,0},{2,3},{3,2},{4,5},{5,4},{6,7},{7,6},{8,9},{9,8},{10,11... | collective-permute-start | bytes 56 | tf_op jit(solution)/shard_map/ppermute | solution.py:386
  2.1 4.5 %collective-permute-start = (f32[1,4]{1,0:T(1,128)}, f32[1,4]{1,0:T(1,128)S(1)}, u32[]{:S(2)}, u32[]{:S(2)}) collective-permute-start(f32[1,4]{1,0:T(1,128)} %param.5), channel_id=1, source_target_pairs={{0,1},{1,0},{2,3},{3,2},{4,5},{5,4},{6,7},{7,6},{8,9},{9,8},{10,11... | collective-permute-start | bytes 56 | tf_op jit(solution)/shard_map/ppermute | solution.py:386
  2.1 4.5 %copy-start = (s32[1,4]{1,0:T(1,128)S(1)}, s32[1,4]{1,0:T(1,128)}, u32[]{:S(2)}) copy-start(s32[1,4]{1,0:T(1,128)} %picks.1) | copy-start | bytes 52
  2.1 4.5 %copy-start.2 = (f32[1,4]{1,0:T(1,128)S(1)}, f32[1,4]{1,0:T(1,128)}, u32[]{:S(2)}) copy-start(f32[1,4]{1,0:T(1,128)} %param.5) | copy-start | bytes 52
  6.7 7.3 %collective-permute-start.2 = (f32[2,8]{1,0:T(2,128)S(1)}, f32[2,8]{1,0:T(2,128)S(1)}, u32[]{:S(2)}, u32[]{:S(2)}) collective-permute-start(f32[2,8]{1,0:T(2,128)S(1)} %pad_maximum_fusion.2.rows), channel_id=1, source_target_pairs={{0,2},{1,3},{2,0},{3,1},{4,6},{5,7},{6,4},{7,5},{8,10},{9,11},{10,... | collective-permute-start | bytes 200 | tf_op jit(solution)/shard_map/ppermute | solution.py:388
  14.0 8.1 %collective-permute-start.3 = (f32[4,8]{1,0:T(4,128)S(1)}, f32[4,8]{1,0:T(4,128)S(1)}, u32[]{:S(2)}, u32[]{:S(2)}) collective-permute-start(f32[4,8]{1,0:T(4,128)S(1)} %pad_maximum_fusion), channel_id=1, source_target_pairs={{0,4},{1,5},{2,6},{3,7},{4,0},{5,1},{6,2},{7,3},{8,12},{9,13},{10,... | collective-permute-start | bytes 392 | tf_op jit(solution)/shard_map/ppermute | solution.py:388
  22.1 19.0 %copy-start.1 = (f32[512,512]{1,0:T(8,128)S(1)}, f32[512,512]{1,0:T(8,128)}, u32[]{:S(2)}) copy-start(f32[512,512]{1,0:T(8,128)} %target.1) | copy-start | bytes 3145732
  39.2 4.1 %collective-permute-start.4 = (f32[512,512]{1,0:T(8,128)S(1)}, f32[512,512]{1,0:T(8,128)S(1)}, u32[]{:S(2)}, u32[]{:S(2)}) collective-permute-start(f32[512,512]{1,0:T(8,128)S(1)} %get-tuple-element.26.run), channel_id=1, source_target_pairs={{0,8},{8,0},{1,9},{9,1},{2,10},{10,2},{3,11},{11,3},{4,12},{12,4},... | collective-permute-start | bytes 3145736 | tf_op jit(solution)/shard_map/ppermute | solution.py:439

commit v7 on v6

--- a/solution.py
+++ b/solution.py
@@ -157,8 +157,10 @@
     copies = [copy(k) for k in range(kinds)] + [last]
     for each in copies:
         each.start()
-    for at in range(0, kinds + 1, 3):
-        group = range(at, min(at + 3, kinds + 1))
+    at = 0
+    while at <= kinds:
+        group = range(at, at + max((kinds + 1 - at) // 2, 1))
+        at = group.stop
         for k in group:
             copies[k].wait()
         for k in group:
@@ -315,11 +317,13 @@
         for c in range(count):
             out[0, c] = jnp.sum(totals[c])
 
-    for rs in pieces(m, 32):
-        gh[rs, :], gl[rs, :] = split(got[rs, :])
+    def receive():
+        for rs in pieces(m, 32):
+            gh[rs, :], gl[rs, :] = split(got[rs, :])
 
     @pl.when(place[0] == 0)
     def _():
+        receive()
         for cs, value in multiply(fh, fl, gh, gl):
             kh[:, cs], kl[:, cs] = split(value)
         for cs, value in multiply_nt(eh, el, kh, kl):
@@ -333,6 +337,7 @@
 
     @pl.when(place[0] != 0)
     def _():
+        receive()
         for cs, value in multiply(eh, el, gh, gl):
             x32[:, cs] = value
         for cs, value in multiply(fh, fl, gh, gl):

time: 48.7 us -> 48.4 us (level)
  transfers between devices with their start and end apart: 5 -> 5, of which waited for: 1 -> 1; matrix products, arithmetic and copies ran while one was open for 0% -> 0% of each run, Pallas kernels for 37% -> 36%
where the time goes in v7:
time: 48.4 us; the launch traced here: 48.3 us
  Pallas kernels  39.6 us (82%)
  starting transfers between devices  7.76 us (16%)
    pallas_call x1, Pallas kernels, on_device(): pl.pallas_call(kernel, out_shape=outs, in_specs=[SMEM] * 2 + [VMEM] * len...  17.1 us
    pallas_call x2, Pallas kernels, on_device(): pl.pallas_call(functools.partial(build_kernel, bit - width), out_shape=(p...  11.5 us
    pallas_call x1, Pallas kernels, on_device(): pl.pallas_call(final_kernel, out_shape=jax.ShapeDtypeStruct((1, count), f...  4.92 us
    pallas_call x1, Pallas kernels, on_device(): pl.pallas_call(load_kernel, out_shape=pltpu.VMEM((kinds + 1, m, m), f32),...  4.14 us
    ppermute x2, starting transfers between devices, on_device(): coming = lax.ppermute(rows, 'fine', swap)  3.82 us
    ppermute x2, starting transfers between devices, on_device(): lax.ppermute((amplitudes, control_index), 'fine', swap)  2.08 us
    pallas_call x1, Pallas kernels, on_device(): pl.pallas_call(functools.partial(turn_kernel, order // 2), out_shape=(hal...  1.91 us
    ppermute x1, starting transfers between devices, on_device(): got = lax.ppermute(run, 'coarse', [(0, 1), (1, 0)])  1.87 us
  transfers between devices with their start and end apart: 5, of which 1 were waited for; matrix products, arithmetic and copies ran while one was open for 0% of the time, Pallas kernels for 36%

profile of v7, /device:TPU:1, one launch (start us, length us, event | category | flops | bytes accessed | tf_op | source)
XLA Modules:
  0.0 48.3 jit_solution(2721186141612005660)
XLA Ops:
  0.0 2.1 %collective-permute-start.1 = (s32[1,4]{1,0:T(1,128)}, s32[1,4]{1,0:T(1,128)S(1)}, u32[]{:S(2)}, u32[]{:S(2)}) collective-permute-start(s32[1,4]{1,0:T(1,128)} %picks.1), channel_id=1, source_target_pairs={{0,1},{1,0},{2,3},{3,2},{4,5},{5,4},{6,7},{7,6},{8,9},{9,8},{10,11... | collective-permute-start | bytes 56 | tf_op jit(solution)/shard_map/ppermute | solution.py:391
  2.1 0.0 collective-permute-start
  2.1 0.0 copy-start
  2.1 4.1 %load.1.table = f32[9,512,512]{2,1,0:T(8,128)S(1)} custom-call(f32[8,512,512]{2,1,0:T(8,128)} %controls.1, f32[512,512]{1,0:T(8,128)} %drift.1), custom_call_target="tpu_custom_call" | custom-call | flops 1610612736 | bytes 6291456 | tf_op jit(solution)/shard_map/load/pallas_call | solution.py:395
  6.2 0.1 pad_add_fusion.1.place
  6.3 0.0 collective-permute-done.1
  6.3 0.0 copy-done
  6.3 0.0 collective-permute-done
  6.3 0.0 copy-done.2
  6.4 0.1 pad_maximum_fusion.2.rows
  6.5 1.5 %collective-permute-start.2 = (f32[2,8]{1,0:T(2,128)S(1)}, f32[2,8]{1,0:T(2,128)S(1)}, u32[]{:S(2)}, u32[]{:S(2)}) collective-permute-start(f32[2,8]{1,0:T(2,128)S(1)} %pad_maximum_fusion.2.rows), channel_id=1, source_target_pairs={{0,2},{1,3},{2,0},{3,1},{4,6},{5,7},{6,4},{7,5},{8,10},{9,11},{10,... | collective-permute-start | bytes 200 | tf_op jit(solution)/shard_map/ppermute | solution.py:393
  8.0 5.8 %build.2 = (bf16[4,512,512]{2,1,0:T(8,128)(2,1)S(1)}, bf16[4,512,512]{2,1,0:T(8,128)(2,1)S(1)}) custom-call(f32[2,8]{1,0:T(2,128)S(1)} %pad_maximum_fusion.2.rows, f32[9,512,512]{2,1,0:T(8,128)S(1)} %load.1.table), custom_call_target="tpu_custom_call" | custom-call | flops 6442450944 | bytes 25165824 | tf_op jit(solution)/shard_map/build/pallas_call | solution.py:407
  13.7 0.0 collective-permute-done.2.rows
  13.7 0.1 pad_maximum_fusion
  13.8 2.3 %collective-permute-start.3 = (f32[4,8]{1,0:T(4,128)S(1)}, f32[4,8]{1,0:T(4,128)S(1)}, u32[]{:S(2)}, u32[]{:S(2)}) collective-permute-start(f32[4,8]{1,0:T(4,128)S(1)} %pad_maximum_fusion), channel_id=1, source_target_pairs={{0,4},{1,5},{2,6},{3,7},{4,0},{5,1},{6,2},{7,3},{8,12},{9,13},{10,... | collective-permute-start | bytes 392 | tf_op jit(solution)/shard_map/ppermute | solution.py:393
  16.1 5.8 %build.3 = (bf16[4,512,512]{2,1,0:T(8,128)(2,1)S(1)}, bf16[4,512,512]{2,1,0:T(8,128)(2,1)S(1)}) custom-call(f32[2,8]{1,0:T(2,128)S(1)} %collective-permute-done.2.rows, f32[9,512,512]{2,1,0:T(8,128)S(1)} %load.1.table, bf16[4,512,512]{2,1,0:T(8,128)(2,1)S(1)} %get-tuple-element.22.refs_0_, ...), custom_call_target="tpu_custom_call", output_to_operand_aliasing={{0}: (2, {}), {1}: (3, {})} | custom-call | flops 6442450944 | bytes 25165824 | tf_op jit(solution)/shard_map/build/pallas_call | solution.py:407
  21.9 0.0 collective-permute-done.3.rows
  21.9 0.0 copy-start.1
  21.9 17.1 %chain.1 = (f32[512,512]{1,0:T(8,128)S(1)}, bf16[512,512]{1,0:T(8,128)(2,1)S(1)}, bf16[512,512]{1,0:T(8,128)(2,1)S(1)}, bf16[512,512]{1,0:T(8,128)(2,1)S(1)}, bf16[512,512]{1,0:T(8,128)(2,1)S(1)}) custom-call(s32[2]{0:T(128)S(1)} %pad_add_fusion.1.place, f32[4,8]{1,0:T(4,128)S(1)} %collective-permute-done.3.rows, f32[9,512,512]{2,1,0:T(8,128)S(1)} %load.1.table, ...), custom_call_target="tpu_custom_call" | custom-call | flops 18522046464 | bytes 72351744 | tf_op jit(solution)/shard_map/chain/pallas_call | solution.py:434
  39.0 1.9 %collective-permute-start.4 = (f32[512,512]{1,0:T(8,128)S(1)}, f32[512,512]{1,0:T(8,128)S(1)}, u32[]{:S(2)}, u32[]{:S(2)}) collective-permute-start(f32[512,512]{1,0:T(8,128)S(1)} %get-tuple-element.26.run), channel_id=1, source_target_pairs={{0,8},{8,0},{1,9},{9,1},{2,10},{10,2},{3,11},{11,3},{4,12},{12,4},... | collective-permute-start | bytes 3145736 | tf_op jit(solution)/shard_map/ppermute | solution.py:444
  40.9 0.0 copy-done.1
  40.9 1.9 %turn.1 = (bf16[512,512]{1,0:T(8,128)(2,1)S(1)}, bf16[512,512]{1,0:T(8,128)(2,1)S(1)}, bf16[512,512]{1,0:T(8,128)(2,1)S(1)}, bf16[512,512]{1,0:T(8,128)(2,1)S(1)}) custom-call(s32[2]{0:T(128)S(1)} %pad_add_fusion.1.place, f32[512,512]{1,0:T(8,128)S(1)} %get-tuple-element.26.run, f32[512,512]{1,0:T(8,128)S(1)} %copy-done.1, ...), custom_call_target="tpu_custom_call" | custom-call | flops 1610612736 | bytes 6291456 | tf_op jit(solution)/shard_map/turn/pallas_call | solution.py:445
  42.8 0.4 collective-permute-done.4.got
  43.2 4.9 %final.1 = f32[1,4]{1,0:T(1,128)} custom-call(s32[2]{0:T(128)S(1)} %pad_add_fusion.1.place, s32[1,4]{1,0:T(1,128)S(1)} %copy-done, f32[512,512]{1,0:T(8,128)S(1)} %collective-permute-done.4.got, bf16[512,512]{1,0:T(8,128)(2,1)S(1)} %get-tuple-element.31.eh, bf16[512,512]{1,0:T(8,128)(2,1)S(1)} %get-tuple-element.32.el, ...), custom_call_target="tpu_custom_call" | custom-call | tf_op jit(solution)/shard_map/final/pallas_call | solution.py:455
  (4 shorter events, 0.0 us)
Async XLA Ops:
  0.0 6.3 %collective-permute-start.1 = (s32[1,4]{1,0:T(1,128)}, s32[1,4]{1,0:T(1,128)S(1)}, u32[]{:S(2)}, u32[]{:S(2)}) collective-permute-start(s32[1,4]{1,0:T(1,128)} %picks.1), channel_id=1, source_target_pairs={{0,1},{1,0},{2,3},{3,2},{4,5},{5,4},{6,7},{7,6},{8,9},{9,8},{10,11... | collective-permute-start | bytes 56 | tf_op jit(solution)/shard_map/ppermute | solution.py:391
  2.1 4.3 %collective-permute-start = (f32[1,4]{1,0:T(1,128)}, f32[1,4]{1,0:T(1,128)S(1)}, u32[]{:S(2)}, u32[]{:S(2)}) collective-permute-start(f32[1,4]{1,0:T(1,128)} %param.5), channel_id=1, source_target_pairs={{0,1},{1,0},{2,3},{3,2},{4,5},{5,4},{6,7},{7,6},{8,9},{9,8},{10,11... | collective-permute-start | bytes 56 | tf_op jit(solution)/shard_map/ppermute | solution.py:391
  2.1 4.2 %copy-start = (s32[1,4]{1,0:T(1,128)S(1)}, s32[1,4]{1,0:T(1,128)}, u32[]{:S(2)}) copy-start(s32[1,4]{1,0:T(1,128)} %picks.1) | copy-start | bytes 52
  2.1 4.3 %copy-start.2 = (f32[1,4]{1,0:T(1,128)S(1)}, f32[1,4]{1,0:T(1,128)}, u32[]{:S(2)}) copy-start(f32[1,4]{1,0:T(1,128)} %param.5) | copy-start | bytes 52
  6.5 7.3 %collective-permute-start.2 = (f32[2,8]{1,0:T(2,128)S(1)}, f32[2,8]{1,0:T(2,128)S(1)}, u32[]{:S(2)}, u32[]{:S(2)}) collective-permute-start(f32[2,8]{1,0:T(2,128)S(1)} %pad_maximum_fusion.2.rows), channel_id=1, source_target_pairs={{0,2},{1,3},{2,0},{3,1},{4,6},{5,7},{6,4},{7,5},{8,10},{9,11},{10,... | collective-permute-start | bytes 200 | tf_op jit(solution)/shard_map/ppermute | solution.py:393
  13.8 8.1 %collective-permute-start.3 = (f32[4,8]{1,0:T(4,128)S(1)}, f32[4,8]{1,0:T(4,128)S(1)}, u32[]{:S(2)}, u32[]{:S(2)}) collective-permute-start(f32[4,8]{1,0:T(4,128)S(1)} %pad_maximum_fusion), channel_id=1, source_target_pairs={{0,4},{1,5},{2,6},{3,7},{4,0},{5,1},{6,2},{7,3},{8,12},{9,13},{10,... | collective-permute-start | bytes 392 | tf_op jit(solution)/shard_map/ppermute | solution.py:393
  21.9 19.0 %copy-start.1 = (f32[512,512]{1,0:T(8,128)S(1)}, f32[512,512]{1,0:T(8,128)}, u32[]{:S(2)}) copy-start(f32[512,512]{1,0:T(8,128)} %target.1) | copy-start | bytes 3145732
  39.0 4.2 %collective-permute-start.4 = (f32[512,512]{1,0:T(8,128)S(1)}, f32[512,512]{1,0:T(8,128)S(1)}, u32[]{:S(2)}, u32[]{:S(2)}) collective-permute-start(f32[512,512]{1,0:T(8,128)S(1)} %get-tuple-element.26.run), channel_id=1, source_target_pairs={{0,8},{8,0},{1,9},{9,1},{2,10},{10,2},{3,11},{11,3},{4,12},{12,4},... | collective-permute-start | bytes 3145736 | tf_op jit(solution)/shard_map/ppermute | solution.py:444
